TPU v7x, 128 devices: a whole 4x4x4 slice. The times are simulated.
128 devices in a mesh: row: 16 (over x, z), col: 8 (over y, core).
Axes of the slice: x: 4, y: 4, z: 4, core: 2. Of those that a mesh axis runs over, the one named last changes fastest.
Arguments:
- tokens: bfloat16 [384, 8192], P('col', 'row'), may hold values from -6 to 6
- gate_weight: bfloat16 [8192, 26624], P('row', 'col'), may hold values from -0.09375 to 0.09375
- up_weight: bfloat16 [8192, 26624], P('row', 'col'), may hold values from -0.09375 to 0.09375
- down_weight: bfloat16 [26624, 8192], P('col', 'row'), may hold values from -0.0546875 to 0.0546875
- gate_mask: int32 [64, 208], P('row', 'col'), may hold values from 0 to 1, as said below
- up_mask: int32 [64, 208], P('row', 'col'), may hold values from 0 to 1, as said below
- down_mask: int32 [208, 64], P('col', 'row'), may hold values from 0 to 1, as said below
- out_grad: bfloat16 [384, 8192], P('col', 'row'), may hold values from -6 to 6
Outputs:
- mixed_out: bfloat16 [384, 8192], P('col', 'row')
- grad_gate: bfloat16 [8192, 26624], P('row', 'col')
- grad_up: bfloat16 [8192, 26624], P('row', 'col')
- grad_down: bfloat16 [26624, 8192], P('col', 'row')
- input_grad: bfloat16 [384, 8192], P('col', 'row')
Inputs may be any that keep to these rules, and one draw needn't show every extreme that they name: `gate_mask`: 1 keeps a tile of 128 x 128 weights, 0 drops it; the share kept differs between rows of tiles. `up_mask`: 1 keeps a tile of 128 x 128 weights, 0 drops it; the share kept differs between rows of tiles. `down_mask`: 1 keeps a tile of 128 x 128 weights, 0 drops it; the share kept differs between columns of tiles.
All inputs are finite; a program needn't handle non-finite values.
Results may differ from a plain program's by a relative error of at most 0.0049.
Values may be sent and summed in bfloat16 or wider, within the bound.
A program may use at most 128 MiB of HBM per device.

v0:
```python
import jax
import jax.numpy as jnp
from jax import lax
from jax.sharding import PartitionSpec as P


def expand(weight, mask):
    rows_w, cols_w = weight.shape
    tile_size = rows_w // mask.shape[0]
    blocks = weight.reshape(mask.shape[0], tile_size, mask.shape[1], tile_size)
    kept = mask.astype(weight.dtype)[:, None, :, None]
    return (blocks * kept).reshape(rows_w, cols_w)


def contract_last(left, right):
    return lax.dot_general(
        left, right, (((1,), (1,)), ((), ())), preferred_element_type=jnp.float32
    )


def contract_first(left, right):
    return lax.dot_general(
        left, right, (((0,), (0,)), ((), ())), preferred_element_type=jnp.float32
    )


def column_sums(term_fn, row_total):
    return lax.psum_scatter(
        term_fn(jnp.int32(0), row_total * lax.axis_size("col")),
        "col",
        scatter_dimension=0,
        tiled=True,
    )


def body(tokens, gate_weight, up_weight, down_weight, gate_mask, up_mask, down_mask, out_grad):
    tok_all, grad_all = (
        lax.all_gather(tokens, "col", axis=0, tiled=True),
        lax.all_gather(out_grad, "col", axis=0, tiled=True),
    )
    w_pair = jnp.concatenate([expand(gate_weight, gate_mask), expand(up_weight, up_mask)], axis=1)
    w_down = expand(down_weight, down_mask)
    half_width = gate_weight.shape[1]
    row_share = tok_all.shape[0] // lax.axis_size("row")
    row_begin = lax.axis_index("row") * row_share
    col_share = tokens.shape[0]
    pair_sums = lax.psum(jnp.dot(tok_all, w_pair, preferred_element_type=jnp.float32), "row")
    gate_every = pair_sums[:, :half_width]
    hidden_all = (gate_every * jax.nn.sigmoid(gate_every) * pair_sums[:, half_width:]).astype(
        jnp.bfloat16
    )
    pre_mine = lax.dynamic_slice_in_dim(pair_sums, row_begin, row_share, 0)
    gate_mine = pre_mine[:, :half_width]
    up_mine = pre_mine[:, half_width:]

    def down_terms(row_start, row_count):
        return jnp.dot(hidden_all, w_down, preferred_element_type=jnp.float32)

    mixed_out = column_sums(down_terms, col_share).astype(jnp.bfloat16)
    hidden_grad = lax.psum_scatter(
        contract_last(grad_all, w_down), "row", scatter_dimension=0, tiled=True
    )
    sigmoid_gate = jax.nn.sigmoid(gate_mine)
    silu_gate = gate_mine * sigmoid_gate
    gate_grad = (
        hidden_grad * up_mine * sigmoid_gate * (1.0 + gate_mine * (1.0 - sigmoid_gate))
    ).astype(jnp.bfloat16)
    up_grad = (hidden_grad * silu_gate).astype(jnp.bfloat16)
    grad_pair = lax.all_gather(
        jnp.concatenate([gate_grad, up_grad], axis=1), "row", axis=0, tiled=True
    )
    weight_pair = contract_first(tok_all, grad_pair)
    grad_gate = expand(weight_pair[:, :half_width], gate_mask).astype(jnp.bfloat16)
    grad_up = expand(weight_pair[:, half_width:], up_mask).astype(jnp.bfloat16)
    grad_down = expand(contract_first(hidden_all, grad_all), down_mask).astype(jnp.bfloat16)

    def input_terms(row_start, row_count):
        return contract_last(grad_pair, w_pair)

    input_grad = column_sums(input_terms, col_share).astype(jnp.bfloat16)
    return (mixed_out, grad_gate, grad_up, grad_down, input_grad)


def solution(mesh):
    in_specs = (
        P("col", "row"),
        P("row", "col"),
        P("row", "col"),
        P("col", "row"),
        P("row", "col"),
        P("row", "col"),
        P("col", "row"),
        P("col", "row"),
    )
    out_specs = (
        P("col", "row"),
        P("row", "col"),
        P("row", "col"),
        P("col", "row"),
        P("col", "row"),
    )
    return jax.shard_map(body, mesh=mesh, in_specs=in_specs, out_specs=out_specs, check_vma=False)
```

profile of v0, /device:TPU:1, one launch (start us, length us, event | category | flops | bytes accessed | tf_op | source)
XLA Modules:
  0.0 426.7 jit_solution(9403428548975660801)
XLA Ops:
  9.0 4.2 copy.42
  13.3 5.6 %copy.44 = bf16[512,3328]{0,1:T(8,128)(2,1)} copy(bf16[512,3328]{1,0:T(8,128)(2,1)} %param.10) | data formatting | bytes 6815744 | tf_op args[2]
  18.8 15.9 %all_gather.9 = bf16[384,512]{1,0:T(8,128)(2,1)} all-gather(bf16[48,512]{1,0:T(8,128)(2,1)S(1)} %copy-done.11), channel_id=1, replica_groups=mesh['row'=16,'col'=8] {'col'}, dimensions={0}, use_global_device_ids=true | all-gather | bytes 442368 | tf_op jit(solution)/shard_map/all_gather | solution.py:38
  34.8 13.0 %all_gather.10 = bf16[384,512]{1,0:T(8,128)(2,1)S(1)} all-gather(bf16[48,512]{1,0:T(8,128)(2,1)S(1)} %copy-done.12), channel_id=1, replica_groups=mesh['row'=16,'col'=8] {'col'}, dimensions={0}, use_global_device_ids=true | all-gather | bytes 442368 | tf_op jit(solution)/shard_map/all_gather | solution.py:39
  47.8 0.9 mul.96
  48.8 0.9 mul.93
  49.9 1.2 bitcast_multiply_fusion.4
  51.2 10.4 %convolution_bitcast_fusion.1 = f32[384,6656]{1,0:T(8,128)} fusion(bf16[384,512]{1,0:T(8,128)(2,1)S(1)} %copy-done.9, bf16[512,3328]{0,1:T(8,128)(2,1)S(1)} %get-tuple-element.37, bf16[512,3328]{0,1:T(8,128)(2,1)S(1)} %get-tuple-element.38), kind=kOutput, calls=%fused_computation.1 | convolution fusion | flops 2630877184 | bytes 17432576 | tf_op jit(solution)/shard_map/dot_general | solution.py:47
  61.6 0.9 mul.101
  62.6 1.0 copy-done.3
  63.6 4.3 %convolution_bitcast_fusion.2 = f32[384,3328]{0,1:T(8,128)} fusion(bf16[384,512]{1,0:T(8,128)(2,1)S(1)} %all_gather.10, bf16[3328,512]{1,0:T(8,128)(2,1)S(1)} %copy-done.3, bf16[416,8,4,128]{3,2,1,0:T(4,128)(2,1)S(1)} %bitcast.60), kind=kOutput, calls=%fused_computation.9 | convolution fusion | flops 1310326784 | bytes 12320768 | tf_op jit(solution)/shard_map/dot_general | solution.py:16
  69.8 205.1 %all-reduce.4.cloned.1.call-done = (f32[384,6656]{1,0:T(8,128)}, f32[384,3328]{0,1:T(8,128)}) async-done(((f32[384,6656]{1,0:T(8,128)}, f32[384,3328]{0,1:T(8,128)}), (f32[384,6656]{1,0:T(8,128)}, f32[384,3328]{0,1:T(8,128)})) %all-reduce.4.cloned.1.call-update) | async-done | bytes 15335440 | tf_op jit(solution)/shard_map/psum | solution.py:47
  274.9 3.7 constant_dynamic-slice_fusion
  278.6 2.7 copy.47
  281.2 4.9 %fusion.3 = bf16[384,3328]{1,0:T(8,128)(2,1)S(1)} fusion(f32[384,6656]{1,0:T(8,128)} %get-tuple-element.25), kind=kLoop, calls=%fused_computation.11 | loop fusion | flops 7667712 | bytes 12779520 | tf_op jit(solution)/shard_map/convert_element_type | solution.py:49
  286.1 1.5 copy-done
  287.5 2.5 fusion.5
  290.1 1.3 fusion.8
  292.6 0.9 mul.117
  293.5 0.8 copy-done.1
  294.3 3.7 fusion
  298.1 21.1 %reduce-scatter.4.cloned.1.call-done = f32[48,512]{1,0:T(8,128)} async-done(((f32[384,512]{1,0:T(8,128)}), f32[48,512]{1,0:T(8,128)}) %reduce-scatter.4.cloned.1.call-update) | async-done | bytes 98320 | tf_op jit(solution)/shard_map/reduce_scatter | solution.py:28
  319.1 1.5 convert_element_type.46
  320.7 57.7 %all-gather.2.cloned.1.call-done = bf16[384,6656]{1,0:T(8,128)(2,1)} async-done(((bf16[24,6656]{1,0:T(8,128)(2,1)}), bf16[384,6656]{1,0:T(8,128)(2,1)}) %all-gather.2.cloned.1.call-update) | async-done | bytes 5111824 | tf_op jit(solution)/shard_map/all_gather | solution.py:69
  378.4 8.2 %fusion.4 = f32[384,512]{1,0:T(8,128)} fusion(bf16[384,6656]{1,0:T(8,128)(2,1)} %all-gather.2.cloned.1.call-done, bf16[512,3328]{0,1:T(8,128)(2,1)} %copy-done.7, bf16[512,3328]{0,1:T(8,128)(2,1)} %copy-done.8), kind=kOutput, calls=%fused_computation.12 | convolution fusion | flops 2630877184 | bytes 12713984 | tf_op jit(solution)/shard_map/dot_general | solution.py:16
  386.6 5.7 %convolution_bitcast_fusion = f32[512,6656]{0,1:T(8,128)S(1)} fusion(bf16[384,6656]{1,0:T(8,128)(2,1)} %all-gather.2.cloned.1.call-done, bf16[384,512]{1,0:T(8,128)(2,1)S(1)} %copy-done.10), kind=kOutput, calls=%fused_computation | convolution fusion | flops 2617245696 | bytes 19136512 | tf_op jit(solution)/shard_map/dot_general | solution.py:22
  392.4 3.8 mul.111
  396.2 3.8 mul.114
  400.0 9.7 %fusion.1 = (bf16[512,3328]{0,1:T(8,128)(2,1)S(1)}, bf16[512,3328]{0,1:T(8,128)(2,1)}) fusion(f32[416,8,4,128]{3,2,1,0:T(4,128)} %bitcast.59, f32[512,6656]{0,1:T(8,128)S(1)} %convolution_bitcast_fusion, f32[416,8,4,128]{3,2,1,0:T(4,128)} %bitcast.58), kind=kLoop, calls=%fused_computation.5 | loop fusion | flops 6815744 | bytes 34078720 | tf_op jit(solution)/shard_map/convert_element_type | solution.py:74
  409.6 5.5 %copy.52 = bf16[512,3328]{1,0:T(8,128)(2,1)} copy(bf16[512,3328]{0,1:T(8,128)(2,1)} %get-tuple-element.28) | data formatting | bytes 6815744
  415.2 3.5 copy.53
  418.7 1.5 convert_element_type.55
  (47 shorter events, 4.6 us)
Async XLA Ops:
  7.2 267.7 %all-reduce.4.cloned.1.call-start = ((), (), s32[]{:S(2)}) async-start(), calls=%async_computation.5 | async-start | bytes 30670848 | tf_op jit(solution)/shard_map/psum | solution.py:47
  13.2 5.6 %copy-start.11 = (bf16[48,512]{1,0:T(8,128)(2,1)S(1)}, bf16[48,512]{1,0:T(8,128)(2,1)}, u32[]{:S(2)}) copy-start(bf16[48,512]{1,0:T(8,128)(2,1)} %param.8) | copy-start | bytes 147460
  13.2 21.5 %copy-start.13 = (s32[26,4]{0,1:T(4,128)S(1)}, s32[26,4]{0,1:T(4,128)}, u32[]{:S(2)}) copy-start(s32[26,4]{0,1:T(4,128)} %param.14) | copy-start | bytes 1252
  13.2 21.6 %copy-start.12 = (bf16[48,512]{1,0:T(8,128)(2,1)S(1)}, bf16[48,512]{1,0:T(8,128)(2,1)}, u32[]{:S(2)}) copy-start(bf16[48,512]{1,0:T(8,128)(2,1)} %param.15) | copy-start | bytes 147460
  47.8 14.7 %copy-start.5 = (bf16[384,512]{1,0:T(8,128)(2,1)}, bf16[384,512]{1,0:T(8,128)(2,1)S(1)}, u32[]{:S(2)}) copy-start(bf16[384,512]{1,0:T(8,128)(2,1)S(1)} %all_gather.10) | copy-start | bytes 1179652
  47.8 2.1 copy-start.2
  49.9 1.3 copy-start.9
  51.2 10.4 %copy-start.7 = (bf16[512,3328]{0,1:T(8,128)(2,1)}, bf16[512,3328]{0,1:T(8,128)(2,1)S(1)}, u32[]{:S(2)}) copy-start(bf16[512,3328]{0,1:T(8,128)(2,1)S(1)} %get-tuple-element.37) | copy-start | bytes 10223620
  51.2 10.4 %copy-start.8 = (bf16[512,3328]{0,1:T(8,128)(2,1)}, bf16[512,3328]{0,1:T(8,128)(2,1)S(1)}, u32[]{:S(2)}) copy-start(bf16[512,3328]{0,1:T(8,128)(2,1)S(1)} %get-tuple-element.38) | copy-start | bytes 10223620
  61.6 2.0 copy-start.3
  67.9 0.7 copy-start.14
  67.9 251.2 %reduce-scatter.4.cloned.1.call-start = ((), (), s32[]{:S(2)}) async-start(), calls=%async_computation.2 | async-start | bytes 884736 | tf_op jit(solution)/shard_map/reduce_scatter | solution.py:28
  281.2 6.3 %copy-start.4 = (bf16[3328,512]{1,0:T(8,128)(2,1)S(1)}, bf16[3328,512]{1,0:T(8,128)(2,1)}, u32[]{:S(2)}) copy-start(bf16[3328,512]{1,0:T(8,128)(2,1)} %param.11) | copy-start | bytes 10223620
  286.1 1.5 copy-start
  290.1 88.4 %all-gather.2.cloned.1.call-start = ((), (), s32[]{:S(2)}) async-start(), calls=%async_computation.3 | async-start | bytes 5431296 | tf_op jit(solution)/shard_map/all_gather | solution.py:69
  292.2 126.4 %reduce-scatter.6.cloned.1.call-start = ((), (), s32[]{:S(2)}) async-start(), calls=%async_computation.4 | async-start | bytes 884736 | tf_op jit(solution)/shard_map/reduce_scatter | solution.py:28
  292.6 1.7 copy-start.1
  292.6 1.8 copy-start.6
  320.7 65.9 %copy-start.10 = (bf16[384,512]{1,0:T(8,128)(2,1)S(1)}, bf16[384,512]{1,0:T(8,128)(2,1)}, u32[]{:S(2)}) copy-start(bf16[384,512]{1,0:T(8,128)(2,1)} %all_gather.9) | copy-start | bytes 1179652
Sparse Core Ops, SparseCore 0:
  68.0 206.7 all-reduce.3
  290.2 28.9 reduce-scatter.3
  321.3 57.0 all-gather.1
  386.7 28.8 reduce-scatter.5
where the time goes:
time: 427 us
  waiting for transfers between devices  284 us (67%)
  local copies, waits for them, and re-layouts  41.7 us (10%)
  matrix products  34.8 us (8%)
  blocking collectives  28.9 us (7%)
  other arithmetic  22.4 us (5%)
  between operations  14.6 us (3%)
    psum x1, waiting for transfers between devices, body(): lax.psum(jnp.dot(tok_all, w_pair, preferred_element_type=jnp.float32), 'r...  205 us
    all_gather x1, waiting for transfers between devices, body(): lax.all_gather(jnp.concatenate([gate_grad, up_grad], axis=1), 'row', axis...  57.7 us
    unnamed x36, local copies, waits for them, and re-layouts  27 us
    reduce_scatter x2, waiting for transfers between devices, column_sums(): lax.psum_scatter(term_fn(jnp.int32(0), row_total * lax.axis_size('col')),...  21.1 us
    all_gather x1, blocking collectives, body(): lax.all_gather(tokens, 'col', axis=0, tiled=True)  15.9 us
    all_gather x1, blocking collectives, body(): lax.all_gather(out_grad, 'col', axis=0, tiled=True)  13 us
    dot_general x2, matrix products, contract_last(): lax.dot_general(left, right, (((1,), (1,)), ((), ())), preferred_element_...  12.5 us
    mul x6, local copies, waits for them, and re-layouts, expand(): return (blocks * kept).reshape(rows_w, cols_w)  11.4 us
  transfers between devices with their start and end apart: 4, of which 3 were waited for; matrix products, arithmetic and copies ran while one was open for 10% of the time, Pallas kernels for 0%

commit v1 on v0

v1 whole, which is shorter than its diff:
```python
import jax
import jax.numpy as jnp
from jax import lax
from jax.sharding import PartitionSpec as P


def expand(weight, mask):
    rows_w, cols_w = weight.shape
    tile_size = rows_w // mask.shape[0]
    blocks = weight.reshape(mask.shape[0], tile_size, mask.shape[1], tile_size)
    kept = mask.astype(weight.dtype)[:, None, :, None]
    return (blocks * kept).reshape(rows_w, cols_w)


def contract_last(left, right):
    return lax.dot_general(
        left, right, (((1,), (1,)), ((), ())), preferred_element_type=jnp.float32
    )


def contract_first(left, right):
    return lax.dot_general(
        left, right, (((0,), (0,)), ((), ())), preferred_element_type=jnp.float32
    )


def body(tokens, gate_weight, up_weight, down_weight, gate_mask, up_mask, down_mask, out_grad):
    feat = tokens.shape[1]
    both_all = lax.all_gather(
        jnp.concatenate([tokens, out_grad], axis=1), "col", axis=0, tiled=True
    )
    tok_all = both_all[:, :feat]
    grad_all = both_all[:, feat:]
    w_gate = expand(gate_weight, gate_mask)
    w_up = expand(up_weight, up_mask)
    w_down = expand(down_weight, down_mask)

    gate_mine = lax.psum_scatter(
        jnp.dot(tok_all, w_gate, preferred_element_type=jnp.float32),
        "row", scatter_dimension=0, tiled=True,
    )
    up_mine = lax.psum_scatter(
        jnp.dot(tok_all, w_up, preferred_element_type=jnp.float32),
        "row", scatter_dimension=0, tiled=True,
    )
    sigmoid_gate = jax.nn.sigmoid(gate_mine)
    silu_gate = gate_mine * sigmoid_gate
    hidden_mine = (silu_gate * up_mine).astype(jnp.bfloat16)
    hidden_all = lax.all_gather(hidden_mine, "row", axis=0, tiled=True)

    hidden_grad = lax.psum_scatter(
        contract_last(grad_all, w_down), "row", scatter_dimension=0, tiled=True
    )
    gate_grad = (
        hidden_grad * up_mine * sigmoid_gate * (1.0 + gate_mine * (1.0 - sigmoid_gate))
    ).astype(jnp.bfloat16)
    up_grad = (hidden_grad * silu_gate).astype(jnp.bfloat16)
    grad_pair = lax.all_gather(
        jnp.concatenate([gate_grad, up_grad], axis=1), "row", axis=0, tiled=True
    )
    half_width = gate_weight.shape[1]
    weight_pair = contract_first(tok_all, grad_pair)
    grad_gate = expand(weight_pair[:, :half_width], gate_mask).astype(jnp.bfloat16)
    grad_up = expand(weight_pair[:, half_width:], up_mask).astype(jnp.bfloat16)
    grad_down = expand(contract_first(hidden_all, grad_all), down_mask).astype(jnp.bfloat16)

    mixed_part = jnp.dot(hidden_all, w_down, preferred_element_type=jnp.float32)
    input_part = contract_last(grad_pair[:, :half_width], w_gate) + contract_last(
        grad_pair[:, half_width:], w_up
    )
    out_sums = lax.psum_scatter(
        jnp.concatenate([mixed_part, input_part], axis=1), "col", scatter_dimension=0, tiled=True
    )
    mixed_out = out_sums[:, :feat].astype(jnp.bfloat16)
    input_grad = out_sums[:, feat:].astype(jnp.bfloat16)
    return (mixed_out, grad_gate, grad_up, grad_down, input_grad)


def solution(mesh):
    in_specs = (
        P("col", "row"),
        P("row", "col"),
        P("row", "col"),
        P("col", "row"),
        P("row", "col"),
        P("row", "col"),
        P("col", "row"),
        P("col", "row"),
    )
    out_specs = (
        P("col", "row"),
        P("row", "col"),
        P("row", "col"),
        P("col", "row"),
        P("col", "row"),
    )
    return jax.shard_map(body, mesh=mesh, in_specs=in_specs, out_specs=out_specs, check_vma=False)
```

time: 427 us -> 447 us (1.047)
  waiting for transfers between devices: 284 us -> 317 us
  blocking collectives: 28.9 us -> 16.3 us
  other arithmetic: 22.4 us -> 15.5 us
  local copies, waits for them, and re-layouts: 41.7 us -> 47.5 us
    unnamed x4 -> x9, waiting for transfers between devices: 0.07 us -> 221 us
    psum x1 -> x0, waiting for transfers between devices: 205 us -> none  [body(): lax.psum(jnp.dot(tok_all, w_pair, preferred_element_type=jnp.float32), 'r...]
    all_gather x0 -> x1, waiting for transfers between devices: none -> 44.2 us  [body(): hidden_all = lax.all_gather(hidden_mine, 'row', axis=0, tiled=True)]
    reduce_scatter x2 -> x1, waiting for transfers between devices: 21.1 us -> 0.01 us  [body(): lax.psum_scatter(jnp.concatenate([mixed_part, input_part], axis=1), 'col'...]
    all_gather x2 -> x1, blocking collectives: 28.9 us -> 16.3 us  [body(): lax.all_gather(jnp.concatenate([tokens, out_grad], axis=1), 'col', axis=0...]
    mul x6 -> x8, local copies, waits for them, and re-layouts: 11.4 us -> 21 us  [expand(): return (blocks * kept).reshape(rows_w, cols_w)]
    convert_element_type x4 -> x1, other arithmetic: 9.22 us -> 2.11 us  [body(): hidden_mine = (silu_gate * up_mine).astype(jnp.bfloat16)]
    all_gather x1, waiting for transfers between devices: 57.7 us -> 51.6 us  [body(): lax.all_gather(jnp.concatenate([gate_grad, up_grad], axis=1), 'row', axis...]
  transfers between devices with their start and end apart: 4 -> 6, of which waited for: 3 -> 5; matrix products, arithmetic and copies ran while one was open for 10% -> 15% of each run, Pallas kernels for 0% -> 0%
where the time goes in v1:
time: 447 us; the launch traced here: 446 us
  waiting for transfers between devices  317 us (71%)
  local copies, waits for them, and re-layouts  47.5 us (11%)
  matrix products  35.1 us (8%)
  blocking collectives  16.3 us (4%)
  other arithmetic  15.5 us (3%)
  between operations  14.3 us (3%)
    unnamed x9, waiting for transfers between devices  221 us
    all_gather x1, waiting for transfers between devices, body(): lax.all_gather(jnp.concatenate([gate_grad, up_grad], axis=1), 'row', axis...  51.6 us
    all_gather x1, waiting for transfers between devices, body(): hidden_all = lax.all_gather(hidden_mine, 'row', axis=0, tiled=True)  44.2 us
    unnamed x34, local copies, waits for them, and re-layouts  25.3 us
    mul x8, local copies, waits for them, and re-layouts, expand(): return (blocks * kept).reshape(rows_w, cols_w)  21 us
    all_gather x1, blocking collectives, body(): lax.all_gather(jnp.concatenate([tokens, out_grad], axis=1), 'col', axis=0...  16.3 us
    dot_general x3, matrix products, contract_last(): lax.dot_general(left, right, (((1,), (1,)), ((), ())), preferred_element_...  12.7 us
  transfers between devices with their start and end apart: 6, of which 5 were waited for; matrix products, arithmetic and copies ran while one was open for 15% of the time, Pallas kernels for 0%

profile of v1, /device:TPU:1, one launch (start us, length us, event | category | flops | bytes accessed | tf_op | source)
XLA Modules:
  0.0 446.2 jit_solution(16238817399744067588)
XLA Ops:
  8.0 16.3 %all_gather.9 = bf16[384,1024]{1,0:T(8,128)(2,1)} all-gather(bf16[48,1024]{1,0:T(8,128)(2,1)S(1)} %pad_maximum_fusion.2), channel_id=1, replica_groups=mesh['row'=16,'col'=8] {'col'}, dimensions={0}, use_global_device_ids=true | all-gather | bytes 884736 | tf_op jit(solution)/shard_map/all_gather | solution.py:29
  25.2 4.2 copy.26
  29.5 0.9 mul.87
  30.4 1.7 copy-done
  32.2 3.9 fusion.10
  36.8 5.6 %copy.28 = bf16[512,3328]{0,1:T(8,128)(2,1)} copy(bf16[512,3328]{1,0:T(8,128)(2,1)} %param.10) | data formatting | bytes 6815744 | tf_op args[2]
  42.4 0.9 mul.91
  43.4 1.7 copy-done.3
  45.1 4.9 %fusion.11 = f32[384,3328]{1,0:T(8,128)} fusion(bf16[512,3328]{0,1:T(8,128)(2,1)S(1)} %copy-done.2, bf16[416,8,4,128]{3,2,1,0:T(4,128)(2,1)S(1)} %bitcast.53, bf16[384,1024]{1,0:T(8,128)(2,1)} %all_gather.9), kind=kOutput, calls=%fused_computation.18 | convolution fusion | flops 1310326784 | bytes 12320768 | tf_op jit(solution)/shard_map/dot_general | solution.py:43
  50.8 0.9 mul.95
  51.8 1.7 copy-done.4
  53.5 5.9 %fusion.12 = f32[384,3328]{1,0:T(8,128)} fusion(bf16[3328,512]{1,0:T(8,128)(2,1)} %param.11, bf16[416,8,4,128]{3,2,1,0:T(4,128)(2,1)S(1)} %bitcast.55, bf16[384,1024]{1,0:T(8,128)(2,1)S(1)} %copy-done.6), kind=kOutput, calls=%fused_computation.19 | convolution fusion | flops 1310326784 | bytes 12320768 | tf_op jit(solution)/shard_map/dot_general | solution.py:16
  59.4 56.1 %reduce-scatter.13.cloned.1.call-done = f32[24,3328]{1,0:T(8,128)} async-done(((f32[384,3328]{1,0:T(8,128)}), f32[24,3328]{1,0:T(8,128)}) %reduce-scatter.13.cloned.1.call-update) | async-done | bytes 319504
  115.5 82.6 %reduce-scatter.15.cloned.1.call-done = f32[24,3328]{1,0:T(8,128)} async-done(((f32[384,3328]{1,0:T(8,128)}), f32[24,3328]{1,0:T(8,128)}) %reduce-scatter.15.cloned.1.call-update) | async-done | bytes 319504
  198.1 82.6 %reduce-scatter.17.cloned.1.call-done = f32[24,3328]{1,0:T(8,128)} async-done(((f32[384,3328]{1,0:T(8,128)}), f32[24,3328]{1,0:T(8,128)}) %reduce-scatter.17.cloned.1.call-update) | async-done | bytes 319504
  280.7 2.1 multiply_convert_fusion.2
  282.9 1.8 pad_maximum_fusion.1
  284.9 44.2 %all-gather.3.cloned.1.call-done = bf16[384,3328]{1,0:T(8,128)(2,1)} async-done(((bf16[24,3328]{1,0:T(8,128)(2,1)}), bf16[384,3328]{1,0:T(8,128)(2,1)}) %all-gather.3.cloned.1.call-update) | async-done | bytes 2555920 | tf_op jit(solution)/shard_map/all_gather | solution.py:49
  329.1 6.1 %fusion.13 = f32[384,512]{1,0:T(8,128)} fusion(bf16[384,3328]{1,0:T(8,128)(2,1)} %all-gather.3.cloned.1.call-done, bf16[3328,512]{1,0:T(8,128)(2,1)} %param.11, bf16[416,8,4,128]{3,2,1,0:T(4,128)(2,1)} %bitcast.56), kind=kOutput, calls=%fused_computation.20 | convolution fusion | flops 1310326784 | bytes 10158080 | tf_op jit(solution)/shard_map/dot_general | solution.py:67
  335.2 51.6 %all-gather.5.cloned.1.call-done = bf16[384,6656]{1,0:T(8,128)(2,1)} async-done(((bf16[24,6656]{1,0:T(8,128)(2,1)}), bf16[384,6656]{1,0:T(8,128)(2,1)}) %all-gather.5.cloned.1.call-update) | async-done | bytes 5111824 | tf_op jit(solution)/shard_map/all_gather | solution.py:58
  386.8 5.4 %fusion.3 = f32[384,512]{1,0:T(8,128)S(1)} fusion(bf16[384,6656]{1,0:T(8,128)(2,1)} %all-gather.5.cloned.1.call-done, bf16[512,3328]{0,1:T(8,128)(2,1)} %copy.28, bf16[416,8,4,128]{3,2,1,0:T(4,128)(2,1)} %bitcast.54), kind=kOutput, calls=%fused_computation.11 | convolution fusion | flops 1310326784 | bytes 10158080 | tf_op jit(solution)/shard_map/dot_general | solution.py:16
  393.0 1.5 fusion.7
  394.5 1.4 pad_maximum_fusion
  396.0 0.9 mul.103
  397.0 3.6 copy.54
  400.6 7.7 %copy.31 = f32[512,3328]{1,0:T(8,128)} copy(f32[512,3328]{0,1:T(8,128)} %bitcast.48) | data formatting | bytes 13631488 | tf_op jit(solution)/shard_map/mul | solution.py:12
  408.4 0.9 mul.106
  409.3 3.5 copy.53
  412.8 7.7 %copy.33 = f32[512,3328]{1,0:T(8,128)} copy(f32[512,3328]{0,1:T(8,128)} %bitcast.50) | data formatting | bytes 13631488 | tf_op jit(solution)/shard_map/mul | solution.py:12
  422.6 3.8 fusion
  426.3 3.8 fusion.17
  430.1 7.7 %fusion.1 = (bf16[512,3328]{1,0:T(8,128)(2,1)}, bf16[512,3328]{1,0:T(8,128)(2,1)}) fusion(f32[512,3328]{1,0:T(8,128)} %copy.33, f32[512,6656]{1,0:T(8,128)S(1)} %fusion.17, f32[512,3328]{1,0:T(8,128)} %copy.31), kind=kLoop, calls=%fused_computation.5 | loop fusion | flops 6815744 | bytes 34078720 | tf_op jit(solution)/shard_map/convert_element_type | solution.py:64
  (54 shorter events, 8.4 us)
Async XLA Ops:
  7.2 108.3 %reduce-scatter.13.cloned.1.call-start = ((), (), s32[]{:S(2)}) async-start(), calls=%async_computation.7 | async-start | bytes 5431296
  29.5 2.7 copy-start.5
  30.4 1.8 copy-start
  36.0 0.7 copy-start.11
  36.1 162.0 %reduce-scatter.15.cloned.1.call-start = ((), (), s32[]{:S(2)}) async-start(), calls=%async_computation.8 | async-start | bytes 5431296
  42.4 2.7 copy-start.2
  43.4 1.8 copy-start.3
  50.0 0.7 copy-start.12
  50.0 230.7 %reduce-scatter.17.cloned.1.call-start = ((), (), s32[]{:S(2)}) async-start(), calls=%async_computation.9 | async-start | bytes 5431296
  50.8 2.7 copy-start.6
  51.7 1.7 copy-start.4
  59.4 269.7 %all-gather.3.cloned.1.call-start = ((), (), s32[]{:S(2)}) async-start(), calls=%async_computation.4 | async-start | bytes 2715648 | tf_op jit(solution)/shard_map/all_gather | solution.py:49
  282.8 104.0 %all-gather.5.cloned.1.call-start = ((), (), s32[]{:S(2)}) async-start(), calls=%async_computation.5 | async-start | bytes 5431296 | tf_op jit(solution)/shard_map/all_gather | solution.py:58
  284.7 153.1 %reduce-scatter.11.cloned.1.call-start = ((), (), s32[]{:S(2)}) async-start(), calls=%async_computation.6 | async-start | bytes 1769472 | tf_op jit(solution)/shard_map/reduce_scatter | solution.py:71
  386.8 5.4 %copy-start.1 = (bf16[4,128,26,128]{1,0,3,2:T(4,128)(2,1)S(1)}, bf16[4,128,26,128]{1,0,3,2:T(4,128)(2,1)}, u32[]{:S(2)}) copy-start(bf16[4,128,26,128]{1,0,3,2:T(4,128)(2,1)} %copy-done) | copy-start | bytes 10223620
  386.8 6.2 %copy-start.9 = (bf16[384,6656]{1,0:T(8,128)(2,1)S(1)}, bf16[384,6656]{1,0:T(8,128)(2,1)}, u32[]{:S(2)}) copy-start(bf16[384,6656]{1,0:T(8,128)(2,1)} %all-gather.5.cloned.1.call-done) | copy-start | bytes 15335428
  393.0 1.5 copy-start.10
  420.6 1.1 copy-start.7
  420.6 2.0 copy-start.8
  420.6 5.7 %slice-start = ((s8[5111808]{0:T(1024)(128)(4,1)}), s8[4194304]{0:T(1024)(128)(4,1)S(1)}, s32[]{:S(2)}) async-start(s8[5111808]{0:T(1024)(128)(4,1)} %bitcast.57), calls=%async_computation.10 | async-start | bytes 8388608
  422.6 3.8 slice-start.1
Sparse Core Ops, SparseCore 0:
  36.2 79.2 reduce-scatter.12
  118.9 79.1 reduce-scatter.14
  201.4 79.1 reduce-scatter.16
  282.9 46.0 all-gather.2
  331.1 55.6 all-gather.4
  396.1 29.9 reduce-scatter.10

commit v2 on v1

v2 whole, which is shorter than its diff:
```python
import jax
import jax.numpy as jnp
from jax import lax
from jax.sharding import PartitionSpec as P

CHUNKS = 2


def expand(weight, mask):
    rows_w, cols_w = weight.shape
    tile_size = rows_w // mask.shape[0]
    blocks = weight.reshape(mask.shape[0], tile_size, mask.shape[1], tile_size)
    kept = mask.astype(weight.dtype)[:, None, :, None]
    return (blocks * kept).reshape(rows_w, cols_w)


def contract_last(left, right):
    return lax.dot_general(
        left, right, (((1,), (1,)), ((), ())), preferred_element_type=jnp.float32
    )


def contract_first(left, right):
    return lax.dot_general(
        left, right, (((0,), (0,)), ((), ())), preferred_element_type=jnp.float32
    )


def body(tokens, gate_weight, up_weight, down_weight, gate_mask, up_mask, down_mask, out_grad):
    feat = tokens.shape[1]
    both_all = lax.all_gather(
        jnp.concatenate([tokens, out_grad], axis=1), "col", axis=0, tiled=True
    )
    tok_all = both_all[:, :feat]
    grad_all = both_all[:, feat:]
    width = gate_weight.shape[1]
    tile = width // gate_mask.shape[1]
    tiles = gate_mask.shape[1]
    bounds = [tiles * k // CHUNKS for k in range(CHUNKS + 1)]

    gate_parts, up_parts, down_parts = [], [], []
    mixed_part = None
    input_part = None
    prev_sums = None
    for k in range(CHUNKS):
        t0, t1 = bounds[k], bounds[k + 1]
        h0, h1 = t0 * tile, t1 * tile
        g_mask = gate_mask[:, t0:t1]
        u_mask = up_mask[:, t0:t1]
        d_mask = down_mask[t0:t1, :]
        w_gate = expand(gate_weight[:, h0:h1], g_mask)
        w_up = expand(up_weight[:, h0:h1], u_mask)
        w_down = expand(down_weight[h0:h1, :], d_mask)
        n = h1 - h0
        partial = jnp.concatenate(
            [
                jnp.dot(tok_all, w_gate, preferred_element_type=jnp.float32),
                jnp.dot(tok_all, w_up, preferred_element_type=jnp.float32),
                contract_last(grad_all, w_down),
            ],
            axis=1,
        )
        if prev_sums is not None:
            partial, _ = lax.optimization_barrier((partial, prev_sums))
        sums = lax.psum(partial, "row")
        prev_sums = sums
        gate_val = sums[:, :n]
        up_val = sums[:, n : 2 * n]
        hidden_grad = sums[:, 2 * n :]
        sigmoid_gate = jax.nn.sigmoid(gate_val)
        silu_gate = gate_val * sigmoid_gate
        hidden = (silu_gate * up_val).astype(jnp.bfloat16)
        gate_grad = (
            hidden_grad * up_val * sigmoid_gate * (1.0 + gate_val * (1.0 - sigmoid_gate))
        ).astype(jnp.bfloat16)
        up_grad = (hidden_grad * silu_gate).astype(jnp.bfloat16)
        gate_parts.append(expand(contract_first(tok_all, gate_grad), g_mask).astype(jnp.bfloat16))
        up_parts.append(expand(contract_first(tok_all, up_grad), u_mask).astype(jnp.bfloat16))
        down_parts.append(expand(contract_first(hidden, grad_all), d_mask).astype(jnp.bfloat16))
        m = jnp.dot(hidden, w_down, preferred_element_type=jnp.float32)
        i = contract_last(gate_grad, w_gate) + contract_last(up_grad, w_up)
        mixed_part = m if mixed_part is None else mixed_part + m
        input_part = i if input_part is None else input_part + i

    out_sums = lax.psum_scatter(
        jnp.concatenate([mixed_part, input_part], axis=1), "col", scatter_dimension=0, tiled=True
    )
    mixed_out = out_sums[:, :feat].astype(jnp.bfloat16)
    input_grad = out_sums[:, feat:].astype(jnp.bfloat16)
    grad_gate = jnp.concatenate(gate_parts, axis=1)
    grad_up = jnp.concatenate(up_parts, axis=1)
    grad_down = jnp.concatenate(down_parts, axis=0)
    return (mixed_out, grad_gate, grad_up, grad_down, input_grad)


def solution(mesh):
    in_specs = (
        P("col", "row"),
        P("row", "col"),
        P("row", "col"),
        P("col", "row"),
        P("row", "col"),
        P("row", "col"),
        P("col", "row"),
        P("col", "row"),
    )
    out_specs = (
        P("col", "row"),
        P("row", "col"),
        P("row", "col"),
        P("col", "row"),
        P("col", "row"),
    )
    return jax.shard_map(body, mesh=mesh, in_specs=in_specs, out_specs=out_specs, check_vma=False)
```

time: 447 us -> 377 us (0.84)
  waiting for transfers between devices: 317 us -> 222 us
  local copies, waits for them, and re-layouts: 47.5 us -> 74 us
  matrix products: 35.1 us -> 24 us
  other arithmetic: 15.5 us -> 24.4 us
    unnamed x9 -> x3, waiting for transfers between devices: 221 us -> 0.05 us
    psum x0 -> x2, waiting for transfers between devices: none -> 210 us  [body(): sums = lax.psum(partial, 'row')]
    all_gather x2 -> x0, waiting for transfers between devices: 95.8 us -> none  [the longest x1 51.6 us: body(): lax.all_gather(jnp.concatenate([gate_grad, up_grad], axis=1), 'row', axis...]
    unnamed x34 -> x88, local copies, waits for them, and re-layouts: 25.3 us -> 39.6 us
    reduce_scatter x1, waiting for transfers between devices: 0.01 us -> 11.7 us  [body(): lax.psum_scatter(jnp.concatenate([mixed_part, input_part], axis=1), 'col'...]
    concatenate x1 -> x4, other arithmetic: 1.76 us -> 11.8 us  [the longest x2 6.74 us: body(): jnp.concatenate([jnp.dot(tok_all, w_gate, preferred_element_type=jnp.floa...]
    slice x0 -> x2, local copies, waits for them, and re-layouts: none -> 7.39 us  [the longest x1 3.97 us: body(): w_up = expand(up_weight[:, h0:h1], u_mask)]
    dot_general x3 -> x6, matrix products: 12.7 us -> 7.49 us  [contract_last(): lax.dot_general(left, right, (((1,), (1,)), ((), ())), preferred_element_...]
  transfers between devices with their start and end apart: 6 -> 3, of which waited for: 5 -> 3; matrix products, arithmetic and copies ran while one was open for 15% -> 19% of each run, Pallas kernels for 0% -> 0%
where the time goes in v2:
time: 377 us; the launch traced here: 374 us
  waiting for transfers between devices  222 us (59%)
  local copies, waits for them, and re-layouts  74 us (20%)
  other arithmetic  24.4 us (6%)
  matrix products  24 us (6%)
  blocking collectives  15.2 us (4%)
  between operations  14.3 us (4%)
    psum x2, waiting for transfers between devices, body(): sums = lax.psum(partial, 'row')  210 us
    unnamed x88, local copies, waits for them, and re-layouts  39.6 us
    mul x16, local copies, waits for them, and re-layouts, expand(): return (blocks * kept).reshape(rows_w, cols_w)  25.3 us
    all_gather x1, blocking collectives, body(): lax.all_gather(jnp.concatenate([tokens, out_grad], axis=1), 'col', axis=0...  15.2 us
    reduce_scatter x1, waiting for transfers between devices, body(): lax.psum_scatter(jnp.concatenate([mixed_part, input_part], axis=1), 'col'...  11.7 us
    dot_general x6, matrix products, contract_first(): lax.dot_general(left, right, (((0,), (0,)), ((), ())), preferred_element_...  10 us
    convert_element_type x2, other arithmetic, body(): hidden = (silu_gate * up_val).astype(jnp.bfloat16)  8.56 us
  transfers between devices with their start and end apart: 3, of which 3 were waited for; matrix products, arithmetic and copies ran while one was open for 19% of the time, Pallas kernels for 0%

profile of v2, /device:TPU:1, one launch (start us, length us, event | category | flops | bytes accessed | tf_op | source)
XLA Modules:
  0.0 374.2 jit_solution(8029856646719886359)
XLA Ops:
  8.0 15.2 %all_gather.3 = bf16[384,1024]{1,0:T(8,128)(2,1)S(1)} all-gather(bf16[48,1024]{1,0:T(8,128)(2,1)S(1)} %pad_maximum_fusion.6), channel_id=1, replica_groups=mesh['row'=16,'col'=8] {'col'}, dimensions={0}, use_global_device_ids=true | all-gather | bytes 884736 | tf_op jit(solution)/shard_map/all_gather | solution.py:31
  24.2 3.4 fusion.26
  27.6 2.3 copy.37
  30.1 4.0 %fusion.27 = (bf16[512,1664]{1,0:T(8,128)(2,1)}, bf16[512,1664]{1,0:T(8,128)(2,1)}) fusion(bf16[512,3328]{1,0:T(8,128)(2,1)} %param.10), kind=kLoop, calls=%fused_computation.73 | loop fusion | bytes 6815744 | tf_op jit(solution)/shard_map/slice | solution.py:52
  34.0 2.8 copy.38
  41.7 1.2 copy-done.11
  43.9 3.3 pad_maximum_fusion
  47.4 3.7 copy.40
  51.2 3.6 copy.39
  56.6 2.9 fusion.13
  64.7 3.4 pad_maximum_fusion.1
  68.1 115.2 %all-reduce.3.cloned.1.call-done = f32[384,4992]{1,0:T(8,128)} async-done(((f32[384,4992]{1,0:T(8,128)}), f32[384,4992]{1,0:T(8,128)}) %all-reduce.3.cloned.1.call-update) | async-done | bytes 7667728 | tf_op jit(solution)/shard_map/psum | solution.py:65
  184.1 2.1 copy.77
  186.2 4.8 %copy.34 = f32[512,1664]{1,0:T(8,128)} copy(f32[512,1664]{0,1:T(8,128)} %bitcast.101) | data formatting | bytes 6815744 | tf_op jit(solution)/shard_map/mul | solution.py:14
  191.6 2.1 copy.79
  193.7 4.8 %copy.30 = f32[512,1664]{1,0:T(8,128)} copy(f32[512,1664]{0,1:T(8,128)} %bitcast.103) | data formatting | bytes 6815744 | tf_op jit(solution)/shard_map/mul | solution.py:14
  199.1 2.1 copy.78
  201.2 4.9 %copy.32 = f32[512,1664]{1,0:T(8,128)} copy(f32[512,1664]{0,1:T(8,128)} %bitcast.105) | data formatting | bytes 6815744 | tf_op jit(solution)/shard_map/mul | solution.py:14
  206.7 2.1 copy.80
  208.8 4.8 %copy.28 = f32[512,1664]{1,0:T(8,128)} copy(f32[512,1664]{0,1:T(8,128)} %bitcast.107) | data formatting | bytes 6815744 | tf_op jit(solution)/shard_map/mul | solution.py:14
  213.7 4.3 %multiply_convert_fusion.9 = (bf16[384,1664]{1,0:T(8,128)(2,1)S(1)}, bf16[384,1664]{1,0:T(8,128)(2,1)S(1)}, bf16[384,1664]{1,0:T(8,128)(2,1)S(1)}) fusion(f32[384,4992]{1,0:T(8,128)} %all-reduce.3.cloned.1.call-done), kind=kLoop, calls=%fused_computation.24 | loop fusion | flops 9584640 | bytes 11501568 | tf_op jit(solution)/shard_map/convert_element_type | solution.py:72
  219.4 1.9 copy-done.6
  221.3 2.4 multiply_convert_fusion.1
  224.6 1.8 fusion.17
  226.4 95.0 %all-reduce.5.cloned.1.call-done = f32[384,4992]{1,0:T(8,128)} async-done(((f32[384,4992]{1,0:T(8,128)}), f32[384,4992]{1,0:T(8,128)}) %all-reduce.5.cloned.1.call-update) | async-done | bytes 7667728 | tf_op jit(solution)/shard_map/psum | solution.py:65
  321.4 4.3 %multiply_convert_fusion.8 = (bf16[384,1664]{1,0:T(8,128)(2,1)S(1)}, bf16[384,1664]{1,0:T(8,128)(2,1)S(1)}, bf16[384,1664]{1,0:T(8,128)(2,1)S(1)}) fusion(f32[384,4992]{1,0:T(8,128)} %all-reduce.5.cloned.1.call-done), kind=kLoop, calls=%fused_computation.21 | loop fusion | flops 9584640 | bytes 11501568 | tf_op jit(solution)/shard_map/convert_element_type | solution.py:72
  327.2 1.3 copy-done.20
  334.5 1.3 pad_maximum_fusion.5
  336.3 3.1 multiply_convert_fusion.3
  349.1 2.0 pad_maximum_fusion.4
  351.3 3.1 pad_maximum_fusion.2
  354.4 11.7 %reduce-scatter.2.cloned.1.call-done = f32[48,1024]{1,0:T(8,128)} async-done(((f32[384,1024]{1,0:T(8,128)}), f32[48,1024]{1,0:T(8,128)}) %reduce-scatter.2.cloned.1.call-update) | async-done | bytes 196624 | tf_op jit(solution)/shard_map/reduce_scatter | solution.py:85
  (127 shorter events, 39.1 us)
Async XLA Ops:
  7.2 176.1 %all-reduce.3.cloned.1.call-start = ((), (), s32[]{:S(2)}) async-start(), calls=%async_computation.1 | async-start | bytes 15335424 | tf_op jit(solution)/shard_map/psum | solution.py:65
  27.6 2.3 copy-start.37
  34.0 2.9 copy-start.38
  37.1 1.5 copy-start.7
  37.6 1.9 copy-start.9
  40.0 2.9 copy-start.34
  47.3 274.1 %all-reduce.5.cloned.1.call-start = ((), (), s32[]{:S(2)}) async-start(), calls=%async_computation.2 | async-start | bytes 15335424 | tf_op jit(solution)/shard_map/psum | solution.py:65
  60.1 1.9 copy-start.15
  62.0 1.7 copy-start.17
  183.3 182.8 %reduce-scatter.2.cloned.1.call-start = ((), (), s32[]{:S(2)}) async-start(), calls=%async_computation.3 | async-start | bytes 1769472 | tf_op jit(solution)/shard_map/reduce_scatter | solution.py:85
  213.7 4.3 %copy-start.8 = (bf16[512,1664]{0,1:T(8,128)(2,1)S(1)}, bf16[512,1664]{0,1:T(8,128)(2,1)}, u32[]{:S(2)}) copy-start(bf16[512,1664]{0,1:T(8,128)(2,1)} %copy.37) | copy-start | bytes 5111812
  213.7 4.5 %copy-start.10 = (bf16[4,128,13,128]{1,0,3,2:T(4,128)(2,1)S(1)}, bf16[4,128,13,128]{1,0,3,2:T(4,128)(2,1)}, u32[]{:S(2)}) copy-start(bf16[4,128,13,128]{1,0,3,2:T(4,128)(2,1)} %copy-done.9) | copy-start | bytes 5111812
  218.0 1.5 copy-start.2
  218.0 5.7 %copy-start.24 = (bf16[384,1664]{1,0:T(8,128)(2,1)}, bf16[384,1664]{1,0:T(8,128)(2,1)S(1)}, u32[]{:S(2)}) copy-start(bf16[384,1664]{1,0:T(8,128)(2,1)S(1)} %get-tuple-element.10) | copy-start | bytes 3833860
  218.2 3.1 copy-start.6
  221.3 2.4 copy-start.12
  221.3 3.2 copy-start.35
  321.3 4.4 %copy-start.18 = (bf16[512,1664]{0,1:T(8,128)(2,1)S(1)}, bf16[512,1664]{0,1:T(8,128)(2,1)}, u32[]{:S(2)}) copy-start(bf16[512,1664]{0,1:T(8,128)(2,1)} %copy.39) | copy-start | bytes 5111812
  321.3 4.4 %copy-start.22 = (bf16[4,128,13,128]{1,0,3,2:T(4,128)(2,1)S(1)}, bf16[4,128,13,128]{1,0,3,2:T(4,128)(2,1)}, u32[]{:S(2)}) copy-start(bf16[4,128,13,128]{1,0,3,2:T(4,128)(2,1)} %copy-done.21) | copy-start | bytes 5111812
  325.7 1.5 copy-start.28
  325.7 5.0 %copy-start.32 = (bf16[384,1664]{1,0:T(8,128)(2,1)}, bf16[384,1664]{1,0:T(8,128)(2,1)S(1)}, u32[]{:S(2)}) copy-start(bf16[384,1664]{1,0:T(8,128)(2,1)S(1)} %get-tuple-element.9) | copy-start | bytes 3833860
  325.7 2.7 copy-start.20
  325.7 3.8 %copy-start.36 = (bf16[3328,512]{1,0:T(8,128)(2,1)S(1)}, bf16[3328,512]{1,0:T(8,128)(2,1)}, u32[]{:S(2)}) copy-start(bf16[3328,512]{1,0:T(8,128)(2,1)} %param.11) | copy-start | bytes 10223620
  325.7 4.0 %copy-start.39 = (f32[384,512]{1,0:T(8,128)S(1)}, f32[384,512]{1,0:T(8,128)}, u32[]{:S(2)}) copy-start(f32[384,512]{1,0:T(8,128)} %fusion.17) | copy-start | bytes 2359300
  329.7 2.0 copy-start.16
  331.7 1.8 copy-start.3
  334.5 1.9 copy-start.27
  340.7 2.0 copy-start.4
  340.7 2.3 copy-start.33
  343.1 2.1 copy-start.5
  343.1 2.5 copy-start.31
  349.1 2.2 copy-start.23
  (11 other events, 14.1 us)
Sparse Core Ops, SparseCore 0:
  47.4 135.8 all-reduce.2
  186.8 134.5 all-reduce.4
  335.9 30.0 reduce-scatter.1

commit v3 on v2

--- a/solution.py
+++ b/solution.py
@@ -3,7 +3,7 @@
 from jax import lax
 from jax.sharding import PartitionSpec as P
 
-CHUNKS = 2
+CHUNKS = 1
 
 
 def expand(weight, mask):
@@ -12,6 +12,14 @@
     blocks = weight.reshape(mask.shape[0], tile_size, mask.shape[1], tile_size)
     kept = mask.astype(weight.dtype)[:, None, :, None]
     return (blocks * kept).reshape(rows_w, cols_w)
+
+
+def expand_flat(values, mask):
+    rows_v, cols_v = values.shape
+    rep_r = rows_v // mask.shape[0]
+    rep_c = cols_v // mask.shape[1]
+    kept = jnp.repeat(jnp.repeat(mask.astype(values.dtype), rep_r, axis=0), rep_c, axis=1)
+    return values * kept
 
 
 def contract_last(left, right):
@@ -74,9 +82,9 @@
             hidden_grad * up_val * sigmoid_gate * (1.0 + gate_val * (1.0 - sigmoid_gate))
         ).astype(jnp.bfloat16)
         up_grad = (hidden_grad * silu_gate).astype(jnp.bfloat16)
-        gate_parts.append(expand(contract_first(tok_all, gate_grad), g_mask).astype(jnp.bfloat16))
-        up_parts.append(expand(contract_first(tok_all, up_grad), u_mask).astype(jnp.bfloat16))
-        down_parts.append(expand(contract_first(hidden, grad_all), d_mask).astype(jnp.bfloat16))
+        gate_parts.append(expand_flat(contract_first(tok_all, gate_grad), g_mask).astype(jnp.bfloat16))
+        up_parts.append(expand_flat(contract_first(tok_all, up_grad), u_mask).astype(jnp.bfloat16))
+        down_parts.append(expand_flat(contract_first(hidden, grad_all), d_mask).astype(jnp.bfloat16))
         m = jnp.dot(hidden, w_down, preferred_element_type=jnp.float32)
         i = contract_last(gate_grad, w_gate) + contract_last(up_grad, w_up)
         mixed_part = m if mixed_part is None else mixed_part + m

time: 377 us -> 329 us (0.87)
  local copies, waits for them, and re-layouts: 74 us -> 51.1 us
  waiting for transfers between devices: 222 us -> 207 us
  other arithmetic: 24.4 us -> 16.5 us
    mul x16 -> x3, local copies, waits for them, and re-layouts: 25.3 us -> 2.83 us  [expand(): return (blocks * kept).reshape(rows_w, cols_w)]
    unnamed x88 -> x44, local copies, waits for them, and re-layouts: 39.6 us -> 20.1 us
    reshape x0 -> x2, local copies, waits for them, and re-layouts: none -> 15.4 us  [expand_flat(): jnp.repeat(jnp.repeat(mask.astype(values.dtype), rep_r, axis=0), rep_c, a...]
    reduce_scatter x1, waiting for transfers between devices: 11.7 us -> 0.01 us  [body(): lax.psum_scatter(jnp.concatenate([mixed_part, input_part], axis=1), 'col'...]
    broadcast_in_dim x0 -> x4, local copies, waits for them, and re-layouts: none -> 11.5 us  [the longest x3 11.4 us: expand_flat(): jnp.repeat(jnp.repeat(mask.astype(values.dtype), rep_r, axis=0), rep_c, a...]
    slice x2 -> x0, local copies, waits for them, and re-layouts: 7.39 us -> none  [the longest x1 3.97 us: body(): w_up = expand(up_weight[:, h0:h1], u_mask)]
    dot_general x6 -> x3, matrix products: 10 us -> 15.2 us  [contract_first(): lax.dot_general(left, right, (((0,), (0,)), ((), ())), preferred_element_...]
    concatenate x2 -> x0, other arithmetic: 5.07 us -> none  [the longest x1 3.1 us: body(): grad_gate = jnp.concatenate(gate_parts, axis=1)]
  transfers between devices with their start and end apart: 3 -> 2, of which waited for: 3 -> 1; matrix products, arithmetic and copies ran while one was open for 19% -> 13% of each run, Pallas kernels for 0% -> 0%
where the time goes in v3:
time: 329 us
  waiting for transfers between devices  207 us (63%)
  local copies, waits for them, and re-layouts  51.1 us (16%)
  matrix products  24.4 us (7%)
  other arithmetic  16.5 us (5%)
  blocking collectives  15.2 us (5%)
  between operations  14.3 us (4%)
    psum x1, waiting for transfers between devices, body(): sums = lax.psum(partial, 'row')  207 us
    unnamed x44, local copies, waits for them, and re-layouts  20.1 us
    reshape x2, local copies, waits for them, and re-layouts, expand_flat(): jnp.repeat(jnp.repeat(mask.astype(values.dtype), rep_r, axis=0), rep_c, a...  15.4 us
    all_gather x1, blocking collectives, body(): lax.all_gather(jnp.concatenate([tokens, out_grad], axis=1), 'col', axis=0...  15.2 us
    dot_general x3, matrix products, contract_first(): lax.dot_general(left, right, (((0,), (0,)), ((), ())), preferred_element_...  15.2 us
    broadcast_in_dim x3, local copies, waits for them, and re-layouts, expand_flat(): jnp.repeat(jnp.repeat(mask.astype(values.dtype), rep_r, axis=0), rep_c, a...  11.4 us
    convert_element_type x1, other arithmetic, body(): hidden = (silu_gate * up_val).astype(jnp.bfloat16)  7.03 us
  transfers between devices with their start and end apart: 2, of which 1 were waited for; matrix products, arithmetic and copies ran while one was open for 13% of the time, Pallas kernels for 0%

profile of v3, /device:TPU:1, one launch (start us, length us, event | category | flops | bytes accessed | tf_op | source)
XLA Modules:
  0.0 328.6 jit_solution(15041118080352013411)
XLA Ops:
  7.2 0.8 pad_maximum_fusion.2
  8.0 15.2 %all_gather.3 = bf16[384,1024]{1,0:T(8,128)(2,1)S(1)} all-gather(bf16[48,1024]{1,0:T(8,128)(2,1)S(1)} %pad_maximum_fusion.2), channel_id=1, replica_groups=mesh['row'=16,'col'=8] {'col'}, dimensions={0}, use_global_device_ids=true | all-gather | bytes 884736 | tf_op jit(solution)/shard_map/all_gather | solution.py:39
  24.1 5.6 %copy.16 = bf16[512,3328]{0,1:T(8,128)(2,1)} copy(bf16[512,3328]{1,0:T(8,128)(2,1)} %param.9) | data formatting | bytes 6815744 | tf_op args[1]
  29.8 5.6 %copy.18 = bf16[512,3328]{0,1:T(8,128)(2,1)} copy(bf16[512,3328]{1,0:T(8,128)(2,1)} %param.10) | data formatting | bytes 6815744 | tf_op args[2]
  35.5 0.9 mul.63
  36.5 1.7 copy-done.7
  38.2 1.6 fusion.3
  39.8 0.9 mul.66
  40.8 1.1 copy-done.3
  41.9 1.6 fusion.4
  43.5 0.9 mul.69
  44.4 1.1 copy-done.14
  45.5 1.6 fusion.6
  47.1 5.7 %pad_maximum_fusion = f32[384,9984]{1,0:T(8,128)} fusion(f32[384,3328]{1,0:T(8,128)S(1)} %fusion.6, f32[384,3328]{1,0:T(8,128)S(1)} %fusion.4, f32[384,3328]{1,0:T(8,128)S(1)} %fusion.3), kind=kLoop, calls=%fused_computation | loop fusion | flops 7667712 | bytes 30670848 | tf_op jit(solution)/shard_map/concatenate | solution.py:63
  53.1 206.8 %all-reduce.2.cloned.1.call-done = f32[384,9984]{1,0:T(8,128)} async-done(((f32[384,9984]{1,0:T(8,128)}), f32[384,9984]{1,0:T(8,128)}) %all-reduce.2.cloned.1.call-update) | async-done | bytes 15335440 | tf_op jit(solution)/shard_map/psum | solution.py:73
  259.8 7.0 %multiply_convert_fusion.4 = (bf16[384,3328]{1,0:T(8,128)(2,1)S(1)}, bf16[384,3328]{1,0:T(8,128)(2,1)S(1)}, bf16[384,3328]{1,0:T(8,128)(2,1)S(1)}) fusion(f32[384,9984]{1,0:T(8,128)} %all-reduce.2.cloned.1.call-done), kind=kLoop, calls=%fused_computation.7 | loop fusion | flops 19169280 | bytes 23003136 | tf_op jit(solution)/shard_map/convert_element_type | solution.py:80
  267.3 1.5 fusion.2
  268.8 1.9 copy-done.10
  270.7 1.0 copy-done.15
  271.7 1.5 fusion.5
  273.6 1.0 copy-done.6
  274.7 1.5 convolution_add_fusion
  276.2 1.3 pad_maximum_fusion.1
  277.7 3.8 %broadcast_in_dim.24 = f32[512,26,128]{0,2,1:T(8,128)} broadcast(f32[512,26]{0,1:T(8,128)S(1)} %bitcast.58), dimensions={0,1} | broadcast | bytes 6868992 | tf_op jit(solution)/shard_map/broadcast_in_dim | solution.py:21
  281.5 7.7 %copy.23 = f32[512,3328]{1,0:T(8,128)} copy(f32[512,3328]{0,1:T(8,128)} %bitcast.49) | data formatting | bytes 13631488 | tf_op jit(solution)/shard_map/reshape | solution.py:21
  289.4 3.6 %broadcast_in_dim.22 = f32[512,26,128]{0,2,1:T(8,128)} broadcast(f32[512,26]{0,1:T(8,128)S(1)} %bitcast.59), dimensions={0,1} | broadcast | bytes 6868992 | tf_op jit(solution)/shard_map/broadcast_in_dim | solution.py:21
  293.0 7.7 %copy.21 = f32[512,3328]{1,0:T(8,128)} copy(f32[512,3328]{0,1:T(8,128)} %bitcast.50) | data formatting | bytes 13631488 | tf_op jit(solution)/shard_map/reshape | solution.py:21
  300.8 7.6 %multiply_convert_fusion = bf16[512,3328]{1,0:T(8,128)(2,1)} fusion(f32[512,3328]{1,0:T(8,128)} %copy.23, bf16[384,3328]{1,0:T(8,128)(2,1)} %copy-done.13, bf16[384,1024]{1,0:T(8,128)(2,1)S(1)} %all_gather.3), kind=kOutput, calls=%fused_computation.3 | convolution fusion | flops 1312030720 | bytes 13172736 | tf_op jit(solution)/shard_map/dot_general | solution.py:32
  308.4 3.9 %multiply_convert_fusion.1 = bf16[512,3328]{1,0:T(8,128)(2,1)} fusion(f32[512,3328]{1,0:T(8,128)S(1)} %copy-done, bf16[384,3328]{1,0:T(8,128)(2,1)S(1)} %copy-done.12, bf16[384,1024]{1,0:T(8,128)(2,1)S(1)} %all_gather.3), kind=kOutput, calls=%fused_computation.4 | convolution fusion | flops 1312030720 | bytes 13172736 | tf_op jit(solution)/shard_map/dot_general | solution.py:32
  312.4 4.1 %broadcast_in_dim.26 = f32[3328,4,128]{2,1,0:T(4,128)S(1)} broadcast(f32[3328,4]{1,0:T(8,128)S(1)} %bitcast.57), dimensions={0,1} | broadcast | bytes 6868992 | tf_op jit(solution)/shard_map/broadcast_in_dim | solution.py:21
  316.4 3.7 %fusion = bf16[3328,512]{1,0:T(8,128)(2,1)} fusion(f32[416,8,4,128]{3,2,1,0:T(4,128)S(1)} %bitcast.48, bf16[384,3328]{1,0:T(8,128)(2,1)S(1)} %get-tuple-element.5, bf16[384,1024]{1,0:T(8,128)(2,1)S(1)} %all_gather.3), kind=kOutput, calls=%fused_computation.2 | convolution fusion | flops 1312030720 | bytes 13172736 | tf_op jit(solution)/shard_map/dot_general | solution.py:32
  320.1 0.9 convert.4
  (52 shorter events, 3.5 us)
Async XLA Ops:
  7.2 252.7 %all-reduce.2.cloned.1.call-start = ((), (), s32[]{:S(2)}) async-start(), calls=%async_computation.1 | async-start | bytes 30670848 | tf_op jit(solution)/shard_map/psum | solution.py:73
  24.1 5.6 %copy-start.16 = (s32[4,26]{1,0:T(4,128)S(1)}, s32[4,26]{1,0:T(4,128)}, u32[]{:S(2)}) copy-start(s32[4,26]{1,0:T(4,128)} %param.13) | copy-start | bytes 1252
  29.8 5.6 %copy-start.17 = (s32[26,4]{0,1:T(4,128)S(1)}, s32[26,4]{0,1:T(4,128)}, u32[]{:S(2)}) copy-start(s32[26,4]{0,1:T(4,128)} %param.14) | copy-start | bytes 1252
  35.5 2.7 copy-start.1
  36.5 1.8 copy-start.7
  39.8 2.1 copy-start.3
  40.8 2.7 copy-start.5
  43.5 2.1 copy-start.14
  44.4 2.7 copy-start.9
  52.8 267.3 %reduce-scatter.2.cloned.1.call-start = ((), (), s32[]{:S(2)}) async-start(), calls=%async_computation.2 | async-start | bytes 1769472 | tf_op jit(solution)/shard_map/reduce_scatter | solution.py:93
  259.8 7.1 %copy-start.2 = (bf16[512,3328]{0,1:T(8,128)(2,1)S(1)}, bf16[512,3328]{0,1:T(8,128)(2,1)}, u32[]{:S(2)}) copy-start(bf16[512,3328]{0,1:T(8,128)(2,1)} %copy.16) | copy-start | bytes 10223620
  259.8 7.4 %copy-start.8 = (bf16[4,128,26,128]{1,0,3,2:T(4,128)(2,1)S(1)}, bf16[4,128,26,128]{1,0,3,2:T(4,128)(2,1)}, u32[]{:S(2)}) copy-start(bf16[4,128,26,128]{1,0,3,2:T(4,128)(2,1)} %copy-done.7) | copy-start | bytes 10223620
  266.9 1.9 copy-start.11
  266.9 6.4 %copy-start.13 = (bf16[384,3328]{1,0:T(8,128)(2,1)}, bf16[384,3328]{1,0:T(8,128)(2,1)S(1)}, u32[]{:S(2)}) copy-start(bf16[384,3328]{1,0:T(8,128)(2,1)S(1)} %get-tuple-element.7) | copy-start | bytes 7667716
  267.3 3.4 %copy-start.10 = (bf16[26,128,4,128]{3,2,1,0:T(4,128)(2,1)S(1)}, bf16[26,128,4,128]{3,2,1,0:T(4,128)(2,1)}, u32[]{:S(2)}) copy-start(bf16[26,128,4,128]{3,2,1,0:T(4,128)(2,1)} %copy-done.9) | copy-start | bytes 10223620
  267.3 4.4 %copy-start.15 = (bf16[3328,512]{1,0:T(8,128)(2,1)S(1)}, bf16[3328,512]{1,0:T(8,128)(2,1)}, u32[]{:S(2)}) copy-start(bf16[3328,512]{1,0:T(8,128)(2,1)} %param.11) | copy-start | bytes 10223620
  271.7 2.0 copy-start.4
  271.7 3.0 copy-start.6
  300.8 7.6 %copy-start = (f32[512,3328]{1,0:T(8,128)S(1)}, f32[512,3328]{1,0:T(8,128)}, u32[]{:S(2)}) copy-start(f32[512,3328]{1,0:T(8,128)} %copy.21) | copy-start | bytes 20447236
  300.8 7.6 %copy-start.12 = (bf16[384,3328]{1,0:T(8,128)(2,1)S(1)}, bf16[384,3328]{1,0:T(8,128)(2,1)}, u32[]{:S(2)}) copy-start(bf16[384,3328]{1,0:T(8,128)(2,1)} %copy-done.11) | copy-start | bytes 7667716
Sparse Core Ops, SparseCore 0:
  53.0 206.8 all-reduce.1
  277.6 30.1 reduce-scatter.1

commit v4 on v3

--- a/solution.py
+++ b/solution.py
@@ -18,8 +18,9 @@
     rows_v, cols_v = values.shape
     rep_r = rows_v // mask.shape[0]
     rep_c = cols_v // mask.shape[1]
-    kept = jnp.repeat(jnp.repeat(mask.astype(values.dtype), rep_r, axis=0), rep_c, axis=1)
-    return values * kept
+    kept = jnp.repeat(mask.astype(values.dtype), rep_c, axis=1)
+    blocks = values.reshape(mask.shape[0], rep_r, cols_v)
+    return (blocks * kept[:, None, :]).reshape(rows_v, cols_v)
 
 
 def contract_last(left, right):

time: 329 us -> 318 us (0.967)
  local copies, waits for them, and re-layouts: 51.1 us -> 22.7 us
  waiting for transfers between devices: 207 us -> 225 us
  matrix products: 24.4 us -> 20.5 us
    reduce_scatter x1, waiting for transfers between devices: 0.01 us -> 18 us  [body(): lax.psum_scatter(jnp.concatenate([mixed_part, input_part], axis=1), 'col'...]
    reshape x2 -> x0, local copies, waits for them, and re-layouts: 15.4 us -> none  [expand_flat(): jnp.repeat(jnp.repeat(mask.astype(values.dtype), rep_r, axis=0), rep_c, a...]
    broadcast_in_dim x4 -> x1, local copies, waits for them, and re-layouts: 11.5 us -> 0.08 us  [expand_flat(): kept = jnp.repeat(mask.astype(values.dtype), rep_c, axis=1)]
    dot_general x3, matrix products: 15.2 us -> 11.2 us  [contract_first(): lax.dot_general(left, right, (((0,), (0,)), ((), ())), preferred_element_...]
    unnamed x44 -> x48, local copies, waits for them, and re-layouts: 20.1 us -> 18.7 us
  transfers between devices with their start and end apart: 2 -> 2, of which waited for: 1 -> 2; matrix products, arithmetic and copies ran while one was open for 13% -> 4% of each run, Pallas kernels for 0% -> 0%
where the time goes in v4:
time: 318 us; the launch traced here: 315 us
  waiting for transfers between devices  225 us (71%)
  local copies, waits for them, and re-layouts  22.7 us (7%)
  matrix products  20.5 us (6%)
  other arithmetic  16.6 us (5%)
  blocking collectives  16.3 us (5%)
  between operations  14.4 us (5%)
    psum x1, waiting for transfers between devices, body(): sums = lax.psum(partial, 'row')  207 us
    unnamed x48, local copies, waits for them, and re-layouts  18.7 us
    reduce_scatter x1, waiting for transfers between devices, body(): lax.psum_scatter(jnp.concatenate([mixed_part, input_part], axis=1), 'col'...  18 us
    all_gather x1, blocking collectives, body(): lax.all_gather(jnp.concatenate([tokens, out_grad], axis=1), 'col', axis=0...  16.3 us
    dot_general x3, matrix products, contract_first(): lax.dot_general(left, right, (((0,), (0,)), ((), ())), preferred_element_...  11.2 us
    convert_element_type x1, other arithmetic, body(): hidden = (silu_gate * up_val).astype(jnp.bfloat16)  7.03 us
  transfers between devices with their start and end apart: 2, of which 2 were waited for; matrix products, arithmetic and copies ran while one was open for 4% of the time, Pallas kernels for 0%

profile of v4, /device:TPU:1, one launch (start us, length us, event | category | flops | bytes accessed | tf_op | source)
XLA Modules:
  0.0 315.5 jit_solution(14102845247734505912)
XLA Ops:
  7.2 0.8 pad_maximum_fusion.2
  8.0 16.3 %all_gather.3 = bf16[384,1024]{1,0:T(8,128)(2,1)} all-gather(bf16[48,1024]{1,0:T(8,128)(2,1)S(1)} %pad_maximum_fusion.2), channel_id=1, replica_groups=mesh['row'=16,'col'=8] {'col'}, dimensions={0}, use_global_device_ids=true | all-gather | bytes 884736 | tf_op jit(solution)/shard_map/all_gather | solution.py:40
  24.3 0.8 fusion.18
  25.2 4.3 %copy.16 = bf16[512,3328]{0,1:T(8,128)(2,1)S(1)} copy(bf16[512,3328]{1,0:T(8,128)(2,1)} %param.9) | data formatting | bytes 6815744 | tf_op args[1]
  29.6 5.6 %copy.18 = bf16[512,3328]{0,1:T(8,128)(2,1)} copy(bf16[512,3328]{1,0:T(8,128)(2,1)} %param.10) | data formatting | bytes 6815744 | tf_op args[2]
  35.3 0.9 mul.93
  36.4 1.6 fusion.5
  38.1 0.9 mul.96
  39.1 1.1 copy-done
  40.2 1.6 fusion.6
  41.8 0.9 mul.99
  42.7 1.1 copy-done.16
  43.8 1.6 fusion.8
  45.4 5.7 %pad_maximum_fusion = f32[384,9984]{1,0:T(8,128)} fusion(f32[384,3328]{1,0:T(8,128)S(1)} %fusion.8, f32[384,3328]{1,0:T(8,128)S(1)} %fusion.6, f32[384,3328]{1,0:T(8,128)S(1)} %fusion.5), kind=kLoop, calls=%fused_computation | loop fusion | flops 7667712 | bytes 30670848 | tf_op jit(solution)/shard_map/concatenate | solution.py:64
  51.3 206.7 %all-reduce.2.cloned.1.call-done = f32[384,9984]{1,0:T(8,128)} async-done(((f32[384,9984]{1,0:T(8,128)}), f32[384,9984]{1,0:T(8,128)}) %all-reduce.2.cloned.1.call-update) | async-done | bytes 15335440 | tf_op jit(solution)/shard_map/psum | solution.py:74
  258.1 7.0 %multiply_convert_fusion.2 = (bf16[384,3328]{1,0:T(8,128)(2,1)S(1)}, bf16[384,3328]{1,0:T(8,128)(2,1)S(1)}, bf16[384,3328]{1,0:T(8,128)(2,1)S(1)}) fusion(f32[384,9984]{1,0:T(8,128)} %all-reduce.2.cloned.1.call-done), kind=kLoop, calls=%fused_computation.9 | loop fusion | flops 19169280 | bytes 23003136 | tf_op jit(solution)/shard_map/convert_element_type | solution.py:81
  265.2 1.6 fusion.4
  266.8 0.9 copy-done.10
  267.7 1.9 copy-done.7
  269.6 1.2 copy-done.17
  270.8 1.5 fusion.7
  272.3 0.4 copy-done.1
  272.8 1.0 copy-done.3
  273.8 1.5 convolution_add_fusion
  275.3 1.4 pad_maximum_fusion.1
  277.2 0.6 copy-done.11
  277.9 3.7 %fusion = bf16[3328,512]{1,0:T(8,128)(2,1)} fusion(bf16[384,3328]{1,0:T(8,128)(2,1)S(1)} %copy-done.11, f32[26,512]{1,0:T(8,128)S(1)} %bitcast.59, bf16[384,1024]{1,0:T(8,128)(2,1)S(1)} %copy-done.9), kind=kOutput, calls=%fused_computation.2 | convolution fusion | flops 1312030720 | bytes 6422528 | tf_op jit(solution)/shard_map/dot_general | solution.py:33
  281.6 3.7 %fusion.1 = bf16[512,3328]{1,0:T(8,128)(2,1)} fusion(bf16[384,3328]{1,0:T(8,128)(2,1)S(1)} %copy-done.15, f32[4,3328]{1,0:T(4,128)S(1)} %bitcast.61, bf16[384,1024]{1,0:T(8,128)(2,1)S(1)} %copy-done.9), kind=kOutput, calls=%fused_computation.4 | convolution fusion | flops 1312030720 | bytes 6410240 | tf_op jit(solution)/shard_map/dot_general | solution.py:33
  285.3 3.7 %fusion.2 = bf16[512,3328]{1,0:T(8,128)(2,1)} fusion(bf16[384,3328]{1,0:T(8,128)(2,1)S(1)} %copy-done.13, f32[4,3328]{1,0:T(4,128)S(1)} %bitcast.62, bf16[384,1024]{1,0:T(8,128)(2,1)S(1)} %copy-done.9), kind=kOutput, calls=%fused_computation.6 | convolution fusion | flops 1312030720 | bytes 6410240 | tf_op jit(solution)/shard_map/dot_general | solution.py:33
  289.1 18.0 %reduce-scatter.2.cloned.1.call-done = f32[48,1024]{1,0:T(8,128)} async-done(((f32[384,1024]{1,0:T(8,128)}), f32[48,1024]{1,0:T(8,128)}) %reduce-scatter.2.cloned.1.call-update) | async-done | bytes 196624 | tf_op jit(solution)/shard_map/reduce_scatter | solution.py:94
  307.1 0.9 convert.4
  308.0 0.6 fusion.15
  (49 shorter events, 1.3 us)
Async XLA Ops:
  7.2 250.9 %all-reduce.2.cloned.1.call-start = ((), (), s32[]{:S(2)}) async-start(), calls=%async_computation.1 | async-start | bytes 30670848 | tf_op jit(solution)/shard_map/psum | solution.py:74
  25.2 4.3 %copy-start.18 = (s32[4,26]{1,0:T(4,128)S(1)}, s32[4,26]{1,0:T(4,128)}, u32[]{:S(2)}) copy-start(s32[4,26]{1,0:T(4,128)} %param.13) | copy-start | bytes 1252
  29.6 5.6 %copy-start.19 = (s32[26,4]{0,1:T(4,128)S(1)}, s32[26,4]{0,1:T(4,128)}, u32[]{:S(2)}) copy-start(s32[26,4]{0,1:T(4,128)} %param.14) | copy-start | bytes 1252
  35.3 1.1 copy-start.8
  36.3 1.8 copy-start.4
  38.1 2.1 copy-start
  39.0 2.7 copy-start.2
  41.7 2.1 copy-start.16
  42.7 2.7 copy-start.6
  51.1 256.0 %reduce-scatter.2.cloned.1.call-start = ((), (), s32[]{:S(2)}) async-start(), calls=%async_computation.2 | async-start | bytes 1769472 | tf_op jit(solution)/shard_map/reduce_scatter | solution.py:94
  258.1 7.1 %copy-start.5 = (bf16[4,128,26,128]{1,0,3,2:T(4,128)(2,1)S(1)}, bf16[4,128,26,128]{1,0,3,2:T(4,128)(2,1)}, u32[]{:S(2)}) copy-start(bf16[4,128,26,128]{1,0,3,2:T(4,128)(2,1)} %copy-done.4) | copy-start | bytes 10223620
  265.1 1.6 copy-start.12
  265.1 2.6 copy-start.10
  265.1 7.2 %copy-start.14 = (bf16[384,3328]{1,0:T(8,128)(2,1)}, bf16[384,3328]{1,0:T(8,128)(2,1)S(1)}, u32[]{:S(2)}) copy-start(bf16[384,3328]{1,0:T(8,128)(2,1)S(1)} %get-tuple-element.7) | copy-start | bytes 7667716
  265.1 4.5 %copy-start.7 = (bf16[26,128,4,128]{3,2,1,0:T(4,128)(2,1)S(1)}, bf16[26,128,4,128]{3,2,1,0:T(4,128)(2,1)}, u32[]{:S(2)}) copy-start(bf16[26,128,4,128]{3,2,1,0:T(4,128)(2,1)} %copy-done.6) | copy-start | bytes 10223620
  265.2 5.7 %copy-start.17 = (bf16[3328,512]{1,0:T(8,128)(2,1)S(1)}, bf16[3328,512]{1,0:T(8,128)(2,1)}, u32[]{:S(2)}) copy-start(bf16[3328,512]{1,0:T(8,128)(2,1)} %param.11) | copy-start | bytes 10223620
  270.8 2.0 copy-start.1
  270.8 3.0 copy-start.3
  275.3 1.9 copy-start.9
  275.3 2.5 copy-start.11
  277.0 4.6 %copy-start.15 = (bf16[384,3328]{1,0:T(8,128)(2,1)S(1)}, bf16[384,3328]{1,0:T(8,128)(2,1)}, u32[]{:S(2)}) copy-start(bf16[384,3328]{1,0:T(8,128)(2,1)} %copy-done.14) | copy-start | bytes 7667716
  281.6 3.7 %copy-start.13 = (bf16[384,3328]{1,0:T(8,128)(2,1)S(1)}, bf16[384,3328]{1,0:T(8,128)(2,1)}, u32[]{:S(2)}) copy-start(bf16[384,3328]{1,0:T(8,128)(2,1)} %copy-done.12) | copy-start | bytes 7667716
Sparse Core Ops, SparseCore 0:
  51.2 206.8 all-reduce.1
  276.9 30.1 reduce-scatter.1

commit v5 on v4

--- a/solution.py
+++ b/solution.py
@@ -57,25 +57,19 @@
         g_mask = gate_mask[:, t0:t1]
         u_mask = up_mask[:, t0:t1]
         d_mask = down_mask[t0:t1, :]
-        w_gate = expand(gate_weight[:, h0:h1], g_mask)
-        w_up = expand(up_weight[:, h0:h1], u_mask)
-        w_down = expand(down_weight[h0:h1, :], d_mask)
+        w_gate = expand_flat(gate_weight[:, h0:h1], g_mask)
+        w_up = expand_flat(up_weight[:, h0:h1], u_mask)
+        w_down = expand_flat(down_weight[h0:h1, :], d_mask)
         n = h1 - h0
-        partial = jnp.concatenate(
-            [
-                jnp.dot(tok_all, w_gate, preferred_element_type=jnp.float32),
-                jnp.dot(tok_all, w_up, preferred_element_type=jnp.float32),
-                contract_last(grad_all, w_down),
-            ],
-            axis=1,
+        partial = (
+            jnp.dot(tok_all, w_gate, preferred_element_type=jnp.float32),
+            jnp.dot(tok_all, w_up, preferred_element_type=jnp.float32),
+            contract_last(grad_all, w_down),
         )
         if prev_sums is not None:
             partial, _ = lax.optimization_barrier((partial, prev_sums))
-        sums = lax.psum(partial, "row")
-        prev_sums = sums
-        gate_val = sums[:, :n]
-        up_val = sums[:, n : 2 * n]
-        hidden_grad = sums[:, 2 * n :]
+        gate_val, up_val, hidden_grad = lax.psum(partial, "row")
+        prev_sums = gate_val
         sigmoid_gate = jax.nn.sigmoid(gate_val)
         silu_gate = gate_val * sigmoid_gate
         hidden = (silu_gate * up_val).astype(jnp.bfloat16)

time: 318 us -> 305 us (0.959)
  local copies, waits for them, and re-layouts: 22.7 us -> 6.84 us
  matrix products: 20.5 us -> 27.2 us
    unnamed x48 -> x44, local copies, waits for them, and re-layouts: 18.7 us -> 5.82 us
    concatenate x1 -> x0, other arithmetic: 5.67 us -> none  [body(): jnp.concatenate([jnp.dot(tok_all, w_gate, preferred_element_type=jnp.floa...]
where the time goes in v5:
time: 305 us; the launch traced here: 303 us
  waiting for transfers between devices  225 us (74%)
  matrix products  27.2 us (9%)
  blocking collectives  15.2 us (5%)
  other arithmetic  14.3 us (5%)
  between operations  14.3 us (5%)
  local copies, waits for them, and re-layouts  6.84 us (2%)
    psum x1, waiting for transfers between devices, body(): gate_val, up_val, hidden_grad = lax.psum(partial, 'row')  207 us
    reduce_scatter x1, waiting for transfers between devices, body(): lax.psum_scatter(jnp.concatenate([mixed_part, input_part], axis=1), 'col'...  17.9 us
    all_gather x1, blocking collectives, body(): lax.all_gather(jnp.concatenate([tokens, out_grad], axis=1), 'col', axis=0...  15.2 us
    dot_general x3, matrix products, contract_first(): lax.dot_general(left, right, (((0,), (0,)), ((), ())), preferred_element_...  11.2 us
    convert_element_type x1, other arithmetic, body(): hidden = (silu_gate * up_val).astype(jnp.bfloat16)  7.03 us
    dot_general x3, matrix products, contract_last(): lax.dot_general(left, right, (((1,), (1,)), ((), ())), preferred_element_...  6.95 us
  transfers between devices with their start and end apart: 2, of which 2 were waited for; matrix products, arithmetic and copies ran while one was open for 4% of the time, Pallas kernels for 0%

profile of v5, /device:TPU:1, one launch (start us, length us, event | category | flops | bytes accessed | tf_op | source)
XLA Modules:
  0.0 302.9 jit_solution(1260278809192694951)
XLA Ops:
  7.2 0.8 pad_maximum_fusion.1
  8.0 15.2 %all_gather.3 = bf16[384,1024]{1,0:T(8,128)(2,1)S(1)} all-gather(bf16[48,1024]{1,0:T(8,128)(2,1)S(1)} %pad_maximum_fusion.1), channel_id=1, replica_groups=mesh['row'=16,'col'=8] {'col'}, dimensions={0}, use_global_device_ids=true | all-gather | bytes 884736 | tf_op jit(solution)/shard_map/all_gather | solution.py:40
  23.3 0.8 fusion.14
  24.0 0.1 copy.15
  24.3 0.8 fusion.16
  25.2 2.2 bitcast_multiply_fusion.3
  27.4 3.9 %fusion.5 = f32[384,3328]{1,0:T(8,128)} fusion(bf16[3328,512]{1,0:T(8,128)(2,1)S(1)} %bitcast_multiply_fusion.3, bf16[384,1024]{1,0:T(8,128)(2,1)S(1)} %all_gather.3), kind=kOutput, calls=%fused_computation.17 | convolution fusion | flops 1308622848 | bytes 8912896 | tf_op jit(solution)/shard_map/dot_general | solution.py:27
  31.3 0.1 copy-done.2
  31.4 0.5 copy-done.13
  31.9 0.2 bitcast_multiply_fusion.5
  32.1 0.9 copy-done.5
  33.0 3.7 %fusion.11 = f32[384,3328]{1,0:T(8,128)} fusion(bf16[512,3328]{1,0:T(8,128)(2,1)S(1)} %bitcast_multiply_fusion.5, bf16[384,1024]{1,0:T(8,128)(2,1)S(1)} %copy-done.5), kind=kOutput, calls=%fused_computation.23 | convolution fusion | flops 1308622848 | bytes 8912896 | tf_op jit(solution)/shard_map/dot_general | solution.py:65
  36.9 0.2 bitcast_multiply_fusion.4
  37.1 1.7 copy-done
  38.9 3.8 %fusion.9 = f32[384,3328]{1,0:T(8,128)} fusion(bf16[512,3328]{1,0:T(8,128)(2,1)S(1)} %bitcast_multiply_fusion.4, bf16[384,1024]{1,0:T(8,128)(2,1)S(1)} %copy-done.5), kind=kOutput, calls=%fused_computation.21 | convolution fusion | flops 1308622848 | bytes 8912896 | tf_op jit(solution)/shard_map/dot_general | solution.py:66
  42.7 0.2 reduce-scatter.2.cloned.1.call-start
  43.0 206.8 %all-reduce.3.cloned.1.call-done = (f32[384,3328]{1,0:T(8,128)}, f32[384,3328]{1,0:T(8,128)}, f32[384,3328]{1,0:T(8,128)}) async-done(((f32[384,3328]{1,0:T(8,128)}, f32[384,3328]{1,0:T(8,128)}, f32[384,3328]{1,0:T(8,128)}), (f32[384,3328]{1,0:T(8,128)}, f32[384,3328]{1,0:T(8,128)}, f32[384,3328]{1,0:T(8,128)})) %all-reduce.3.cloned.1.call-update) | async-done | bytes 15335440 | tf_op jit(solution)/shard_map/psum | solution.py:71
  249.8 7.0 %multiply_convert_fusion.2 = (bf16[384,3328]{1,0:T(8,128)(2,1)S(1)}, bf16[384,3328]{1,0:T(8,128)(2,1)S(1)}, bf16[384,3328]{1,0:T(8,128)(2,1)S(1)}) fusion(f32[384,3328]{1,0:T(8,128)} %get-tuple-element.7, f32[384,3328]{1,0:T(8,128)} %get-tuple-element.5, f32[384,3328]{1,0:T(8,128)} %get-tuple-element.6), kind=kLoop, calls=%fused_computation.8 | loop fusion | flops 19169280 | bytes 23003136 | tf_op jit(solution)/shard_map/convert_element_type | solution.py:75
  256.9 1.5 fusion.17
  258.4 0.8 copy-done.9
  259.2 1.5 fusion.18
  260.7 0.6 copy-done.1
  261.3 1.5 convolution_add_fusion
  262.9 1.3 pad_maximum_fusion
  264.2 0.1 copy.16
  264.7 0.7 copy-done.8
  265.4 3.7 %fusion = bf16[3328,512]{1,0:T(8,128)(2,1)} fusion(bf16[384,3328]{1,0:T(8,128)(2,1)S(1)} %copy-done.8, f32[26,512]{1,0:T(8,128)S(1)} %bitcast.56, bf16[384,1024]{1,0:T(8,128)(2,1)S(1)} %copy-done.6), kind=kOutput, calls=%fused_computation.1 | convolution fusion | flops 1312030720 | bytes 6422528 | tf_op jit(solution)/shard_map/dot_general | solution.py:33
  269.1 3.7 %fusion.1 = bf16[512,3328]{1,0:T(8,128)(2,1)} fusion(bf16[384,3328]{1,0:T(8,128)(2,1)S(1)} %copy-done.12, f32[4,3328]{1,0:T(4,128)S(1)} %bitcast.58, bf16[384,1024]{1,0:T(8,128)(2,1)S(1)} %copy-done.6), kind=kOutput, calls=%fused_computation.3 | convolution fusion | flops 1312030720 | bytes 6410240 | tf_op jit(solution)/shard_map/dot_general | solution.py:33
  272.8 3.7 %fusion.2 = bf16[512,3328]{1,0:T(8,128)(2,1)} fusion(bf16[384,3328]{1,0:T(8,128)(2,1)S(1)} %copy-done.10, f32[4,3328]{1,0:T(4,128)S(1)} %bitcast.59, bf16[384,1024]{1,0:T(8,128)(2,1)S(1)} %copy-done.6), kind=kOutput, calls=%fused_computation.5 | convolution fusion | flops 1312030720 | bytes 6410240 | tf_op jit(solution)/shard_map/dot_general | solution.py:33
  276.6 17.9 %reduce-scatter.2.cloned.1.call-done = f32[48,1024]{1,0:T(8,128)} async-done(((f32[384,1024]{1,0:T(8,128)}), f32[48,1024]{1,0:T(8,128)}) %reduce-scatter.2.cloned.1.call-update) | async-done | bytes 196624 | tf_op jit(solution)/shard_map/reduce_scatter | solution.py:88
  294.4 0.9 convert.4
  295.4 0.6 fusion.13
  (43 shorter events, 0.8 us)
Async XLA Ops:
  7.2 242.7 %all-reduce.3.cloned.1.call-start = ((), (), s32[]{:S(2)}) async-start(), calls=%async_computation.2 | async-start | bytes 30670848 | tf_op jit(solution)/shard_map/psum | solution.py:71
  23.3 4.1 %copy-start.4 = (bf16[384,1024]{1,0:T(8,128)(2,1)}, bf16[384,1024]{1,0:T(8,128)(2,1)S(1)}, u32[]{:S(2)}) copy-start(bf16[384,1024]{1,0:T(8,128)(2,1)S(1)} %all_gather.3) | copy-start | bytes 2359300
  27.4 4.1 %copy-start.2 = (bf16[3328,512]{1,0:T(8,128)(2,1)}, bf16[3328,512]{1,0:T(8,128)(2,1)S(1)}, u32[]{:S(2)}) copy-start(bf16[3328,512]{1,0:T(8,128)(2,1)S(1)} %bitcast_multiply_fusion.3) | copy-start | bytes 10223620
  27.4 4.5 %copy-start.13 = (bf16[512,3328]{1,0:T(8,128)(2,1)S(1)}, bf16[512,3328]{1,0:T(8,128)(2,1)}, u32[]{:S(2)}) copy-start(bf16[512,3328]{1,0:T(8,128)(2,1)} %param.9) | copy-start | bytes 10223620
  31.9 1.1 copy-start.5
  33.0 3.7 %copy-start.15 = (s32[4,26]{1,0:T(4,128)S(1)}, s32[4,26]{1,0:T(4,128)}, u32[]{:S(2)}) copy-start(s32[4,26]{1,0:T(4,128)} %param.13) | copy-start | bytes 1252
  33.0 3.8 %copy-start.14 = (bf16[512,3328]{1,0:T(8,128)(2,1)S(1)}, bf16[512,3328]{1,0:T(8,128)(2,1)}, u32[]{:S(2)}) copy-start(bf16[512,3328]{1,0:T(8,128)(2,1)} %param.10) | copy-start | bytes 10223620
  37.1 1.8 copy-start
  42.7 251.7 %reduce-scatter.2.cloned.1.call-start = ((), (), s32[]{:S(2)}) async-start(), calls=%async_computation.1 | async-start | bytes 1769472 | tf_op jit(solution)/shard_map/reduce_scatter | solution.py:88
  249.8 7.1 %copy-start.3 = (bf16[3328,512]{1,0:T(8,128)(2,1)S(1)}, bf16[3328,512]{1,0:T(8,128)(2,1)}, u32[]{:S(2)}) copy-start(bf16[3328,512]{1,0:T(8,128)(2,1)} %copy-done.2) | copy-start | bytes 10223620
  256.9 1.5 copy-start.7
  256.9 2.3 copy-start.9
  256.9 3.8 %copy-start.11 = (bf16[384,3328]{1,0:T(8,128)(2,1)}, bf16[384,3328]{1,0:T(8,128)(2,1)S(1)}, u32[]{:S(2)}) copy-start(bf16[384,3328]{1,0:T(8,128)(2,1)S(1)} %get-tuple-element.10) | copy-start | bytes 7667716
  259.2 2.1 copy-start.1
  262.8 1.8 copy-start.6
  262.8 2.5 copy-start.8
  264.4 4.7 %copy-start.12 = (bf16[384,3328]{1,0:T(8,128)(2,1)S(1)}, bf16[384,3328]{1,0:T(8,128)(2,1)}, u32[]{:S(2)}) copy-start(bf16[384,3328]{1,0:T(8,128)(2,1)} %copy-done.11) | copy-start | bytes 7667716
  269.1 3.7 %copy-start.10 = (bf16[384,3328]{1,0:T(8,128)(2,1)S(1)}, bf16[384,3328]{1,0:T(8,128)(2,1)}, u32[]{:S(2)}) copy-start(bf16[384,3328]{1,0:T(8,128)(2,1)} %copy-done.9) | copy-start | bytes 7667716
Sparse Core Ops, SparseCore 0:
  42.9 206.9 all-reduce.2
  264.3 30.0 reduce-scatter.1

commit v6 on v5

--- a/solution.py
+++ b/solution.py
@@ -70,18 +70,26 @@
             partial, _ = lax.optimization_barrier((partial, prev_sums))
         gate_val, up_val, hidden_grad = lax.psum(partial, "row")
         prev_sums = gate_val
-        sigmoid_gate = jax.nn.sigmoid(gate_val)
-        silu_gate = gate_val * sigmoid_gate
-        hidden = (silu_gate * up_val).astype(jnp.bfloat16)
-        gate_grad = (
-            hidden_grad * up_val * sigmoid_gate * (1.0 + gate_val * (1.0 - sigmoid_gate))
-        ).astype(jnp.bfloat16)
-        up_grad = (hidden_grad * silu_gate).astype(jnp.bfloat16)
+
+        def activations(gate_val, up_val, hidden_grad):
+            sigmoid_gate = jax.nn.sigmoid(gate_val)
+            silu_gate = gate_val * sigmoid_gate
+            hidden = (silu_gate * up_val).astype(jnp.bfloat16)
+            gate_grad = (
+                hidden_grad * up_val * sigmoid_gate * (1.0 + gate_val * (1.0 - sigmoid_gate))
+            ).astype(jnp.bfloat16)
+            up_grad = (hidden_grad * silu_gate).astype(jnp.bfloat16)
+            return hidden, gate_grad, up_grad
+
+        hidden, gate_grad, up_grad = activations(gate_val, up_val, hidden_grad)
+        m = jnp.dot(hidden, w_down, preferred_element_type=jnp.float32)
+        i = contract_last(gate_grad, w_gate) + contract_last(up_grad, w_up)
+        hidden, gate_grad, up_grad = activations(
+            *lax.optimization_barrier((gate_val, up_val, hidden_grad))
+        )
         gate_parts.append(expand_flat(contract_first(tok_all, gate_grad), g_mask).astype(jnp.bfloat16))
         up_parts.append(expand_flat(contract_first(tok_all, up_grad), u_mask).astype(jnp.bfloat16))
         down_parts.append(expand_flat(contract_first(hidden, grad_all), d_mask).astype(jnp.bfloat16))
-        m = jnp.dot(hidden, w_down, preferred_element_type=jnp.float32)
-        i = contract_last(gate_grad, w_gate) + contract_last(up_grad, w_up)
         mixed_part = m if mixed_part is None else mixed_part + m
         input_part = i if input_part is None else input_part + i
 

time: 305 us -> 306 us (level)
  matrix products: 27.2 us -> 45.4 us
  waiting for transfers between devices: 225 us -> 214 us
  other arithmetic: 14.3 us -> 7.24 us
    dot_general x3, matrix products: 11.2 us -> 22.9 us  [contract_first(): lax.dot_general(left, right, (((0,), (0,)), ((), ())), preferred_element_...]
    reduce_scatter x1, waiting for transfers between devices: 17.9 us -> 6.83 us  [body(): lax.psum_scatter(jnp.concatenate([mixed_part, input_part], axis=1), 'col'...]
    convert_element_type x1 -> x0, other arithmetic: 7.03 us -> none  [body(): hidden = (silu_gate * up_val).astype(jnp.bfloat16)]
    dot_general x3, matrix products: 6.95 us -> 13.4 us  [contract_last(): lax.dot_general(left, right, (((1,), (1,)), ((), ())), preferred_element_...]
    unnamed x44 -> x46, local copies, waits for them, and re-layouts: 5.82 us -> 6.63 us
  transfers between devices with their start and end apart: 2 -> 2, of which waited for: 2 -> 2; matrix products, arithmetic and copies ran while one was open for 4% -> 8% of each run, Pallas kernels for 0% -> 0%
where the time goes in v6:
time: 306 us; the launch traced here: 304 us
  waiting for transfers between devices  214 us (70%)
  matrix products  45.4 us (15%)
  blocking collectives  15.2 us (5%)
  between operations  14.3 us (5%)
  local copies, waits for them, and re-layouts  7.66 us (3%)
  other arithmetic  7.24 us (2%)
    psum x1, waiting for transfers between devices, body(): gate_val, up_val, hidden_grad = lax.psum(partial, 'row')  207 us
    dot_general x3, matrix products, contract_first(): lax.dot_general(left, right, (((0,), (0,)), ((), ())), preferred_element_...  22.9 us
    all_gather x1, blocking collectives, body(): lax.all_gather(jnp.concatenate([tokens, out_grad], axis=1), 'col', axis=0...  15.2 us
    dot_general x3, matrix products, contract_last(): lax.dot_general(left, right, (((1,), (1,)), ((), ())), preferred_element_...  13.4 us
    reduce_scatter x1, waiting for transfers between devices, body(): lax.psum_scatter(jnp.concatenate([mixed_part, input_part], axis=1), 'col'...  6.83 us
    unnamed x46, local copies, waits for them, and re-layouts  6.63 us
  transfers between devices with their start and end apart: 2, of which 2 were waited for; matrix products, arithmetic and copies ran while one was open for 8% of the time, Pallas kernels for 0%

profile of v6, /device:TPU:1, one launch (start us, length us, event | category | flops | bytes accessed | tf_op | source)
XLA Modules:
  0.0 303.7 jit_solution(17828575082349016510)
XLA Ops:
  7.2 0.8 pad_maximum_fusion.1
  8.0 15.2 %all_gather.3 = bf16[384,1024]{1,0:T(8,128)(2,1)S(1)} all-gather(bf16[48,1024]{1,0:T(8,128)(2,1)S(1)} %pad_maximum_fusion.1), channel_id=1, replica_groups=mesh['row'=16,'col'=8] {'col'}, dimensions={0}, use_global_device_ids=true | all-gather | bytes 884736 | tf_op jit(solution)/shard_map/all_gather | solution.py:40
  23.3 0.8 fusion.29
  24.0 0.1 copy.15
  24.1 0.1 broadcast_in_dim.20
  24.3 0.8 fusion.30
  25.2 2.2 bitcast_multiply_fusion.3
  27.4 3.9 %fusion.14 = f32[384,3328]{1,0:T(8,128)} fusion(bf16[3328,512]{1,0:T(8,128)(2,1)S(1)} %bitcast_multiply_fusion.3, bf16[384,1024]{1,0:T(8,128)(2,1)S(1)} %all_gather.3), kind=kOutput, calls=%fused_computation.25 | convolution fusion | flops 1308622848 | bytes 8912896 | tf_op jit(solution)/shard_map/dot_general | solution.py:27
  31.3 0.6 copy-done.9
  31.9 0.2 bitcast_multiply_fusion.4
  32.1 0.9 copy-done.7
  33.0 3.8 %fusion.18 = f32[384,3328]{1,0:T(8,128)} fusion(bf16[512,3328]{1,0:T(8,128)(2,1)S(1)} %bitcast_multiply_fusion.4, bf16[384,1024]{1,0:T(8,128)(2,1)S(1)} %copy-done.7), kind=kOutput, calls=%fused_computation.29 | convolution fusion | flops 1308622848 | bytes 8912896 | tf_op jit(solution)/shard_map/dot_general | solution.py:66
  37.0 0.2 bitcast_multiply_fusion.5
  37.2 1.7 copy-done.2
  39.0 3.8 %fusion.20 = f32[384,3328]{1,0:T(8,128)} fusion(bf16[512,3328]{1,0:T(8,128)(2,1)S(1)} %bitcast_multiply_fusion.5, bf16[384,1024]{1,0:T(8,128)(2,1)S(1)} %copy-done.7), kind=kOutput, calls=%fused_computation.31 | convolution fusion | flops 1308622848 | bytes 8912896 | tf_op jit(solution)/shard_map/dot_general | solution.py:65
  42.8 0.2 reduce-scatter.2.cloned.1.call-start
  43.0 206.8 %all-reduce.3.cloned.1.call-done = (f32[384,3328]{1,0:T(8,128)}, f32[384,3328]{1,0:T(8,128)}, f32[384,3328]{1,0:T(8,128)}) async-done(((f32[384,3328]{1,0:T(8,128)}, f32[384,3328]{1,0:T(8,128)}, f32[384,3328]{1,0:T(8,128)}), (f32[384,3328]{1,0:T(8,128)}, f32[384,3328]{1,0:T(8,128)}, f32[384,3328]{1,0:T(8,128)})) %all-reduce.3.cloned.1.call-update) | async-done | bytes 15335440 | tf_op jit(solution)/shard_map/psum | solution.py:71
  249.9 6.5 %fusion.6 = f32[384,512]{1,0:T(8,128)} fusion(bf16[512,3328]{1,0:T(8,128)(2,1)S(1)} %bitcast_multiply_fusion.4, f32[384,3328]{1,0:T(8,128)} %get-tuple-element.8, f32[384,3328]{1,0:T(8,128)} %get-tuple-element.10), kind=kOutput, calls=%fused_computation.20 | convolution fusion | flops 1316290560 | bytes 14417920 | tf_op jit(solution)/shard_map/dot_general | solution.py:27
  256.4 0.7 copy-done.1
  257.1 1.0 copy-done.5
  258.1 1.5 fusion.5
  259.7 1.1 copy-done.3
  260.7 0.1 copy-done.12
  260.9 2.9 fusion.8
  263.8 1.3 pad_maximum_fusion
  265.1 0.1 copy.16
  265.6 8.0 %fusion = bf16[3328,512]{1,0:T(8,128)(2,1)} fusion(f32[26,512]{1,0:T(8,128)S(1)} %bitcast.54, f32[384,3328]{1,0:T(8,128)} %get-tuple-element.9, f32[384,3328]{1,0:T(8,128)} %get-tuple-element.10, bf16[384,1024]{1,0:T(8,128)(2,1)S(1)} %copy-done.8), kind=kOutput, calls=%fused_computation.1 | convolution fusion | flops 1319698432 | bytes 14090240 | tf_op jit(solution)/shard_map/dot_general | solution.py:33
  273.5 6.4 %fusion.1 = bf16[512,3328]{1,0:T(8,128)(2,1)} fusion(f32[4,3328]{1,0:T(4,128)S(1)} %bitcast.56, f32[384,3328]{1,0:T(8,128)} %get-tuple-element.8, f32[384,3328]{1,0:T(8,128)S(1)} %bitcast.51, bf16[384,1024]{1,0:T(8,128)(2,1)S(1)} %copy-done.8), kind=kOutput, calls=%fused_computation.3 | convolution fusion | flops 1319698432 | bytes 14077952 | tf_op jit(solution)/shard_map/dot_general | solution.py:33
  279.9 8.6 %fusion.2 = bf16[512,3328]{1,0:T(8,128)(2,1)} fusion(f32[4,3328]{1,0:T(4,128)S(1)} %bitcast.57, f32[384,3328]{1,0:T(8,128)S(1)} %bitcast.51, f32[384,3328]{1,0:T(8,128)} %get-tuple-element.8, f32[384,3328]{1,0:T(8,128)} %get-tuple-element.9, bf16[384,1024]{1,0:T(8,128)(2,1)S(1)} %copy-done.8), kind=kOutput, calls=%fused_computation.5 | convolution fusion | flops 1324810240 | bytes 19189760 | tf_op jit(solution)/shard_map/dot_general | solution.py:33
  288.5 6.8 %reduce-scatter.2.cloned.1.call-done = f32[48,1024]{1,0:T(8,128)} async-done(((f32[384,1024]{1,0:T(8,128)}), f32[48,1024]{1,0:T(8,128)}) %reduce-scatter.2.cloned.1.call-update) | async-done | bytes 196624 | tf_op jit(solution)/shard_map/reduce_scatter | solution.py:96
  295.3 0.9 convert.4
  296.2 0.6 fusion.28
  (46 shorter events, 0.7 us)
Async XLA Ops:
  7.2 242.7 %all-reduce.3.cloned.1.call-start = ((), (), s32[]{:S(2)}) async-start(), calls=%async_computation.2 | async-start | bytes 30670848 | tf_op jit(solution)/shard_map/psum | solution.py:71
  23.3 8.1 %copy-start.6 = (bf16[384,1024]{1,0:T(8,128)(2,1)}, bf16[384,1024]{1,0:T(8,128)(2,1)S(1)}, u32[]{:S(2)}) copy-start(bf16[384,1024]{1,0:T(8,128)(2,1)S(1)} %all_gather.3) | copy-start | bytes 2359300
  27.4 4.8 %copy-start.4 = (bf16[3328,512]{1,0:T(8,128)(2,1)}, bf16[3328,512]{1,0:T(8,128)(2,1)S(1)}, u32[]{:S(2)}) copy-start(bf16[3328,512]{1,0:T(8,128)(2,1)S(1)} %bitcast_multiply_fusion.3) | copy-start | bytes 10223620
  27.4 4.5 %copy-start.9 = (bf16[512,3328]{1,0:T(8,128)(2,1)S(1)}, bf16[512,3328]{1,0:T(8,128)(2,1)}, u32[]{:S(2)}) copy-start(bf16[512,3328]{1,0:T(8,128)(2,1)} %param.10) | copy-start | bytes 10223620
  31.9 1.1 copy-start.7
  33.0 3.8 %copy-start.11 = (s32[4,26]{1,0:T(4,128)S(1)}, s32[4,26]{1,0:T(4,128)}, u32[]{:S(2)}) copy-start(s32[4,26]{1,0:T(4,128)} %param.12) | copy-start | bytes 1252
  33.0 3.9 %copy-start.10 = (bf16[512,3328]{1,0:T(8,128)(2,1)S(1)}, bf16[512,3328]{1,0:T(8,128)(2,1)}, u32[]{:S(2)}) copy-start(bf16[512,3328]{1,0:T(8,128)(2,1)} %param.9) | copy-start | bytes 10223620
  37.2 1.8 copy-start.2
  42.8 252.5 %reduce-scatter.2.cloned.1.call-start = ((), (), s32[]{:S(2)}) async-start(), calls=%async_computation.1 | async-start | bytes 1769472 | tf_op jit(solution)/shard_map/reduce_scatter | solution.py:96
  249.9 6.6 %copy-start = (f32[384,3328]{1,0:T(8,128)S(1)}, f32[384,3328]{1,0:T(8,128)}, u32[]{:S(2)}) copy-start(f32[384,3328]{1,0:T(8,128)} %get-tuple-element.10) | copy-start | bytes 15335428
  249.9 7.2 %copy-start.1 = (f32[384,3328]{1,0:T(8,128)S(1)}, f32[384,3328]{1,0:T(8,128)}, u32[]{:S(2)}) copy-start(f32[384,3328]{1,0:T(8,128)} %get-tuple-element.9) | copy-start | bytes 15335428
  249.9 8.2 %copy-start.5 = (bf16[3328,512]{1,0:T(8,128)(2,1)S(1)}, bf16[3328,512]{1,0:T(8,128)(2,1)}, u32[]{:S(2)}) copy-start(bf16[3328,512]{1,0:T(8,128)(2,1)} %copy-done.4) | copy-start | bytes 10223620
  249.9 9.7 %slice-start.2 = ((s8[5111808]{0:T(1024)(128)(4,1)}), s8[4194304]{0:T(1024)(128)(4,1)S(1)}, s32[]{:S(2)}) async-start(s8[5111808]{0:T(1024)(128)(4,1)} %bitcast.52), calls=%async_computation.5 | async-start | bytes 8388608
  258.1 1.6 slice-start.3
  258.1 2.7 copy-start.3
  258.1 2.8 copy-start.12
  263.8 1.8 copy-start.8
  265.0 8.5 %slice-start = ((s8[5111808]{0:T(1024)(128)(4,1)}), s8[917504]{0:T(1024)(128)(4,1)S(1)}, s32[]{:S(2)}) async-start(s8[5111808]{0:T(1024)(128)(4,1)} %bitcast.50), calls=%async_computation.3 | async-start | bytes 1835008
  265.6 8.0 %slice-start.1 = ((s8[5111808]{0:T(1024)(128)(4,1)}), s8[4194304]{0:T(1024)(128)(4,1)S(1)}, s32[]{:S(2)}) async-start(s8[5111808]{0:T(1024)(128)(4,1)} %bitcast.50), calls=%async_computation.4 | async-start | bytes 8388608
Sparse Core Ops, SparseCore 0:
  42.9 206.9 all-reduce.2
  265.2 30.0 reduce-scatter.1

commit v7 on v5

--- a/solution.py
+++ b/solution.py
@@ -85,9 +85,10 @@
         mixed_part = m if mixed_part is None else mixed_part + m
         input_part = i if input_part is None else input_part + i
 
-    out_sums = lax.psum_scatter(
-        jnp.concatenate([mixed_part, input_part], axis=1), "col", scatter_dimension=0, tiled=True
-    )
+    both_part = jnp.concatenate([mixed_part, input_part], axis=1)
+    ways = lax.axis_size("col")
+    spread = lax.all_to_all(both_part, "col", 0, 0, tiled=True)
+    out_sums = spread.reshape(ways, spread.shape[0] // ways, spread.shape[1]).sum(axis=0)
     mixed_out = out_sums[:, :feat].astype(jnp.bfloat16)
     input_grad = out_sums[:, feat:].astype(jnp.bfloat16)
     grad_gate = jnp.concatenate(gate_parts, axis=1)

time: 305 us -> 302 us (level)
  waiting for transfers between devices: 225 us -> 216 us
  starting transfers between devices: 0.26 us -> 5.29 us
    reduce_scatter x1 -> x0, waiting for transfers between devices: 17.9 us -> none  [body(): lax.psum_scatter(jnp.concatenate([mixed_part, input_part], axis=1), 'col'...]
    all_to_all x0 -> x1, waiting for transfers between devices: none -> 8.98 us  [body(): spread = lax.all_to_all(both_part, 'col', 0, 0, tiled=True)]
    all_to_all x0 -> x1, starting transfers between devices: none -> 5.26 us  [body(): spread = lax.all_to_all(both_part, 'col', 0, 0, tiled=True)]
where the time goes in v7:
time: 302 us; the launch traced here: 301 us
  waiting for transfers between devices  216 us (72%)
  matrix products  27.2 us (9%)
  blocking collectives  15.2 us (5%)
  other arithmetic  14.8 us (5%)
  between operations  14.3 us (5%)
  local copies, waits for them, and re-layouts  8.18 us (3%)
  starting transfers between devices  5.29 us (2%)
    psum x1, waiting for transfers between devices, body(): gate_val, up_val, hidden_grad = lax.psum(partial, 'row')  207 us
    all_gather x1, blocking collectives, body(): lax.all_gather(jnp.concatenate([tokens, out_grad], axis=1), 'col', axis=0...  15.2 us
    dot_general x3, matrix products, contract_first(): lax.dot_general(left, right, (((0,), (0,)), ((), ())), preferred_element_...  11.2 us
    all_to_all x1, waiting for transfers between devices, body(): spread = lax.all_to_all(both_part, 'col', 0, 0, tiled=True)  8.98 us
    unnamed x44, local copies, waits for them, and re-layouts  7.15 us
    dot_general x3, matrix products, contract_last(): lax.dot_general(left, right, (((1,), (1,)), ((), ())), preferred_element_...  6.96 us
    convert_element_type x1, other arithmetic, body(): hidden = (silu_gate * up_val).astype(jnp.bfloat16)  6.89 us
  transfers between devices with their start and end apart: 2, of which 2 were waited for; matrix products, arithmetic and copies ran while one was open for 4% of the time, Pallas kernels for 0%

profile of v7, /device:TPU:1, one launch (start us, length us, event | category | flops | bytes accessed | tf_op | source)
XLA Modules:
  0.0 301.1 jit_solution(16434013463521125492)
XLA Ops:
  7.2 0.8 pad_maximum_fusion.1
  8.0 15.2 %all_gather.3 = bf16[384,1024]{1,0:T(8,128)(2,1)S(1)} all-gather(bf16[48,1024]{1,0:T(8,128)(2,1)S(1)} %pad_maximum_fusion.1), channel_id=1, replica_groups=mesh['row'=16,'col'=8] {'col'}, dimensions={0}, use_global_device_ids=true | all-gather | bytes 884736 | tf_op jit(solution)/shard_map/all_gather | solution.py:40
  23.3 0.8 fusion.14
  24.0 0.1 copy.15
  24.3 0.8 fusion.16
  25.2 2.2 bitcast_multiply_fusion.3
  27.4 3.9 %fusion.5 = f32[384,3328]{1,0:T(8,128)} fusion(bf16[3328,512]{1,0:T(8,128)(2,1)S(1)} %bitcast_multiply_fusion.3, bf16[384,1024]{1,0:T(8,128)(2,1)S(1)} %all_gather.3), kind=kOutput, calls=%fused_computation.17 | convolution fusion | flops 1308622848 | bytes 8912896 | tf_op jit(solution)/shard_map/dot_general | solution.py:27
  31.3 0.1 copy-done.2
  31.4 0.5 copy-done.13
  31.9 0.2 bitcast_multiply_fusion.5
  32.1 0.9 copy-done.5
  33.0 3.7 %fusion.11 = f32[384,3328]{1,0:T(8,128)} fusion(bf16[512,3328]{1,0:T(8,128)(2,1)S(1)} %bitcast_multiply_fusion.5, bf16[384,1024]{1,0:T(8,128)(2,1)S(1)} %copy-done.5), kind=kOutput, calls=%fused_computation.23 | convolution fusion | flops 1308622848 | bytes 8912896 | tf_op jit(solution)/shard_map/dot_general | solution.py:65
  36.9 0.2 bitcast_multiply_fusion.4
  37.1 1.7 copy-done
  38.9 3.9 %fusion.9 = f32[384,3328]{1,0:T(8,128)} fusion(bf16[512,3328]{1,0:T(8,128)(2,1)S(1)} %bitcast_multiply_fusion.4, bf16[384,1024]{1,0:T(8,128)(2,1)S(1)} %copy-done.5), kind=kOutput, calls=%fused_computation.21 | convolution fusion | flops 1308622848 | bytes 8912896 | tf_op jit(solution)/shard_map/dot_general | solution.py:66
  42.8 207.1 %all-reduce.3.cloned.1.call-done = (f32[384,3328]{1,0:T(8,128)}, f32[384,3328]{1,0:T(8,128)}, f32[384,3328]{1,0:T(8,128)}) async-done(((f32[384,3328]{1,0:T(8,128)}, f32[384,3328]{1,0:T(8,128)}, f32[384,3328]{1,0:T(8,128)}), (f32[384,3328]{1,0:T(8,128)}, f32[384,3328]{1,0:T(8,128)}, f32[384,3328]{1,0:T(8,128)})) %all-reduce.3.cloned.1.call-update) | async-done | bytes 15335440 | tf_op jit(solution)/shard_map/psum | solution.py:71
  249.8 6.9 %multiply_convert_fusion.2 = (bf16[384,3328]{1,0:T(8,128)(2,1)S(1)}, bf16[384,3328]{1,0:T(8,128)(2,1)S(1)}, bf16[384,3328]{1,0:T(8,128)(2,1)S(1)}) fusion(f32[384,3328]{1,0:T(8,128)} %get-tuple-element.7, f32[384,3328]{1,0:T(8,128)} %get-tuple-element.5, f32[384,3328]{1,0:T(8,128)} %get-tuple-element.6), kind=kLoop, calls=%fused_computation.8 | loop fusion | flops 19169280 | bytes 23003136 | tf_op jit(solution)/shard_map/convert_element_type | solution.py:75
  256.8 1.5 fusion.18
  258.3 1.0 copy-done.7
  259.3 1.9 copy-done.3
  261.3 1.5 fusion.17
  262.7 0.5 copy-done.1
  263.2 1.5 convolution_add_fusion
  264.8 1.3 pad_maximum_fusion
  266.1 5.3 %all-to-all-start = ((f32[8,48,1024]{2,1,0:T(8,128)}), f32[8,48,1024]{2,1,0:T(8,128)}, u32[]{:S(2)}, u32[]{:S(2)}) async-start(f32[8,48,1024]{2,1,0:T(8,128)} %bitcast.57), calls=%async_computation | async-start | bytes 3145728 | tf_op jit(solution)/shard_map/all_to_all | solution.py:90
  271.3 0.1 copy.16
  271.8 3.7 %fusion = bf16[3328,512]{1,0:T(8,128)(2,1)} fusion(bf16[384,3328]{1,0:T(8,128)(2,1)S(1)} %copy-done.8, f32[26,512]{1,0:T(8,128)S(1)} %bitcast.58, bf16[384,1024]{1,0:T(8,128)(2,1)S(1)} %copy-done.6), kind=kOutput, calls=%fused_computation.1 | convolution fusion | flops 1312030720 | bytes 6422528 | tf_op jit(solution)/shard_map/dot_general | solution.py:33
  275.6 3.7 %fusion.1 = bf16[512,3328]{1,0:T(8,128)(2,1)} fusion(bf16[384,3328]{1,0:T(8,128)(2,1)S(1)} %copy-done.12, f32[4,3328]{1,0:T(4,128)S(1)} %bitcast.60, bf16[384,1024]{1,0:T(8,128)(2,1)S(1)} %copy-done.6), kind=kOutput, calls=%fused_computation.3 | convolution fusion | flops 1312030720 | bytes 6410240 | tf_op jit(solution)/shard_map/dot_general | solution.py:33
  279.3 3.7 %fusion.2 = bf16[512,3328]{1,0:T(8,128)(2,1)} fusion(bf16[384,3328]{1,0:T(8,128)(2,1)S(1)} %copy-done.10, f32[4,3328]{1,0:T(4,128)S(1)} %bitcast.61, bf16[384,1024]{1,0:T(8,128)(2,1)S(1)} %copy-done.6), kind=kOutput, calls=%fused_computation.5 | convolution fusion | flops 1312030720 | bytes 6410240 | tf_op jit(solution)/shard_map/dot_general | solution.py:33
  283.0 9.0 %all-to-all-done = f32[8,48,1024]{2,1,0:T(8,128)} async-done(((f32[8,48,1024]{2,1,0:T(8,128)}), f32[8,48,1024]{2,1,0:T(8,128)}, u32[]{:S(2)}, u32[]{:S(2)}) %all-to-all-start) | async-done | bytes 1572896 | tf_op jit(solution)/shard_map/all_to_all | solution.py:90
  292.0 1.5 reduce_sum.9
  293.6 0.6 fusion.13
  (42 shorter events, 0.8 us)
Async XLA Ops:
  7.2 242.7 %all-reduce.3.cloned.1.call-start = ((), (), s32[]{:S(2)}) async-start(), calls=%async_computation.1 | async-start | bytes 30670848 | tf_op jit(solution)/shard_map/psum | solution.py:71
  23.3 4.1 %copy-start.4 = (bf16[384,1024]{1,0:T(8,128)(2,1)}, bf16[384,1024]{1,0:T(8,128)(2,1)S(1)}, u32[]{:S(2)}) copy-start(bf16[384,1024]{1,0:T(8,128)(2,1)S(1)} %all_gather.3) | copy-start | bytes 2359300
  27.4 4.1 %copy-start.2 = (bf16[3328,512]{1,0:T(8,128)(2,1)}, bf16[3328,512]{1,0:T(8,128)(2,1)S(1)}, u32[]{:S(2)}) copy-start(bf16[3328,512]{1,0:T(8,128)(2,1)S(1)} %bitcast_multiply_fusion.3) | copy-start | bytes 10223620
  27.4 4.5 %copy-start.13 = (bf16[512,3328]{1,0:T(8,128)(2,1)S(1)}, bf16[512,3328]{1,0:T(8,128)(2,1)}, u32[]{:S(2)}) copy-start(bf16[512,3328]{1,0:T(8,128)(2,1)} %param.9) | copy-start | bytes 10223620
  31.9 1.1 copy-start.5
  33.0 3.7 %copy-start.15 = (s32[4,26]{1,0:T(4,128)S(1)}, s32[4,26]{1,0:T(4,128)}, u32[]{:S(2)}) copy-start(s32[4,26]{1,0:T(4,128)} %param.13) | copy-start | bytes 1252
  33.0 3.8 %copy-start.14 = (bf16[512,3328]{1,0:T(8,128)(2,1)S(1)}, bf16[512,3328]{1,0:T(8,128)(2,1)}, u32[]{:S(2)}) copy-start(bf16[512,3328]{1,0:T(8,128)(2,1)} %param.10) | copy-start | bytes 10223620
  37.1 1.8 copy-start
  256.7 1.6 copy-start.9
  256.7 2.6 copy-start.7
  256.8 6.0 %copy-start.11 = (bf16[384,3328]{1,0:T(8,128)(2,1)}, bf16[384,3328]{1,0:T(8,128)(2,1)S(1)}, u32[]{:S(2)}) copy-start(bf16[384,3328]{1,0:T(8,128)(2,1)S(1)} %get-tuple-element.10) | copy-start | bytes 7667716
  256.8 4.5 %copy-start.3 = (bf16[3328,512]{1,0:T(8,128)(2,1)S(1)}, bf16[3328,512]{1,0:T(8,128)(2,1)}, u32[]{:S(2)}) copy-start(bf16[3328,512]{1,0:T(8,128)(2,1)} %copy-done.2) | copy-start | bytes 10223620
  261.3 2.0 copy-start.1
  264.7 7.1 %copy-start.6 = (bf16[384,1024]{1,0:T(8,128)(2,1)S(1)}, bf16[384,1024]{1,0:T(8,128)(2,1)}, u32[]{:S(2)}) copy-start(bf16[384,1024]{1,0:T(8,128)(2,1)} %copy-done.4) | copy-start | bytes 2359300
  264.7 7.1 %copy-start.8 = (bf16[384,3328]{1,0:T(8,128)(2,1)S(1)}, bf16[384,3328]{1,0:T(8,128)(2,1)}, u32[]{:S(2)}) copy-start(bf16[384,3328]{1,0:T(8,128)(2,1)} %copy-done.7) | copy-start | bytes 7667716
  266.1 25.9 %all-to-all-start = ((f32[8,48,1024]{2,1,0:T(8,128)}), f32[8,48,1024]{2,1,0:T(8,128)}, u32[]{:S(2)}, u32[]{:S(2)}) async-start(f32[8,48,1024]{2,1,0:T(8,128)} %bitcast.57), calls=%async_computation | async-start | bytes 3145728 | tf_op jit(solution)/shard_map/all_to_all | solution.py:90
  271.6 4.0 %copy-start.12 = (bf16[384,3328]{1,0:T(8,128)(2,1)S(1)}, bf16[384,3328]{1,0:T(8,128)(2,1)}, u32[]{:S(2)}) copy-start(bf16[384,3328]{1,0:T(8,128)(2,1)} %copy-done.11) | copy-start | bytes 7667716
  275.6 3.7 %copy-start.10 = (bf16[384,3328]{1,0:T(8,128)(2,1)S(1)}, bf16[384,3328]{1,0:T(8,128)(2,1)}, u32[]{:S(2)}) copy-start(bf16[384,3328]{1,0:T(8,128)(2,1)} %copy-done.9) | copy-start | bytes 7667716
Sparse Core Ops, SparseCore 0:
  42.9 206.9 all-reduce.2

commit v8 on v7

--- a/solution.py
+++ b/solution.py
@@ -50,7 +50,6 @@
     gate_parts, up_parts, down_parts = [], [], []
     mixed_part = None
     input_part = None
-    prev_sums = None
     for k in range(CHUNKS):
         t0, t1 = bounds[k], bounds[k + 1]
         h0, h1 = t0 * tile, t1 * tile
@@ -61,15 +60,20 @@
         w_up = expand_flat(up_weight[:, h0:h1], u_mask)
         w_down = expand_flat(down_weight[h0:h1, :], d_mask)
         n = h1 - h0
-        partial = (
-            jnp.dot(tok_all, w_gate, preferred_element_type=jnp.float32),
-            jnp.dot(tok_all, w_up, preferred_element_type=jnp.float32),
-            contract_last(grad_all, w_down),
+        gate_val, up_val = lax.psum(
+            (
+                jnp.dot(tok_all, w_gate, preferred_element_type=jnp.float32),
+                jnp.dot(tok_all, w_up, preferred_element_type=jnp.float32),
+            ),
+            "row",
         )
-        if prev_sums is not None:
-            partial, _ = lax.optimization_barrier((partial, prev_sums))
-        gate_val, up_val, hidden_grad = lax.psum(partial, "row")
-        prev_sums = gate_val
+        hg_part = contract_last(grad_all, w_down)
+        ways = lax.axis_size("row")
+        rows_all = hg_part.shape[0]
+        hg_spread = lax.all_to_all(hg_part, "row", 0, 0, tiled=True)
+        hg_mine = hg_spread.reshape(ways, rows_all // ways, n).sum(axis=0)
+        hg_rep = jnp.broadcast_to(hg_mine[None], (ways, rows_all // ways, n)).reshape(rows_all, n)
+        hidden_grad = lax.all_to_all(hg_rep, "row", 0, 0, tiled=True)
         sigmoid_gate = jax.nn.sigmoid(gate_val)
         silu_gate = gate_val * sigmoid_gate
         hidden = (silu_gate * up_val).astype(jnp.bfloat16)

time: 302 us -> 349 us (1.16)
  blocking collectives: 15.2 us -> 191 us
  waiting for transfers between devices: 216 us -> 83.8 us
  other arithmetic: 14.8 us -> 20.5 us
    all_to_all x0 -> x2, blocking collectives: none -> 176 us  [the longest x1 101 us: body(): hg_spread = lax.all_to_all(hg_part, 'row', 0, 0, tiled=True)]
    psum x1, waiting for transfers between devices: 207 us -> 74.8 us  [body(): lax.psum((jnp.dot(tok_all, w_gate, preferred_element_type=jnp.float32), j...]
    reduce_sum x0 -> x1, other arithmetic: none -> 3.55 us  [body(): hg_mine = hg_spread.reshape(ways, rows_all // ways, n).sum(axis=0)]
    unnamed x44 -> x40, local copies, waits for them, and re-layouts: 7.15 us -> 6.04 us
  transfers between devices with their start and end apart: 2 -> 2, of which waited for: 2 -> 2; matrix products, arithmetic and copies ran while one was open for 4% -> 6% of each run, Pallas kernels for 0% -> 0%
where the time goes in v8:
time: 349 us
  blocking collectives  191 us (55%)
  waiting for transfers between devices  83.8 us (24%)
  matrix products  24.8 us (7%)
  other arithmetic  20.5 us (6%)
  between operations  14.3 us (4%)
  local copies, waits for them, and re-layouts  8.37 us (2%)
  starting transfers between devices  5.94 us (2%)
    all_to_all x1, blocking collectives, body(): hg_spread = lax.all_to_all(hg_part, 'row', 0, 0, tiled=True)  101 us
    psum x1, waiting for transfers between devices, body(): lax.psum((jnp.dot(tok_all, w_gate, preferred_element_type=jnp.float32), j...  74.8 us
    all_to_all x1, blocking collectives, body(): hidden_grad = lax.all_to_all(hg_rep, 'row', 0, 0, tiled=True)  74.3 us
    all_gather x1, blocking collectives, body(): lax.all_gather(jnp.concatenate([tokens, out_grad], axis=1), 'col', axis=0...  15.2 us
    dot_general x3, matrix products, contract_first(): lax.dot_general(left, right, (((0,), (0,)), ((), ())), preferred_element_...  11.2 us
    all_to_all x1, waiting for transfers between devices, body(): spread = lax.all_to_all(both_part, 'col', 0, 0, tiled=True)  8.98 us
    convert_element_type x1, other arithmetic, body(): hidden = (silu_gate * up_val).astype(jnp.bfloat16)  7.03 us
  transfers between devices with their start and end apart: 2, of which 2 were waited for; matrix products, arithmetic and copies ran while one was open for 6% of the time, Pallas kernels for 0%

profile of v8, /device:TPU:1, one launch (start us, length us, event | category | flops | bytes accessed | tf_op | source)
XLA Modules:
  0.0 348.6 jit_solution(2306819529558114395)
XLA Ops:
  7.2 0.8 pad_maximum_fusion.1
  8.0 15.2 %all_gather.3 = bf16[384,1024]{1,0:T(8,128)(2,1)S(1)} all-gather(bf16[48,1024]{1,0:T(8,128)(2,1)S(1)} %pad_maximum_fusion.1), channel_id=1, replica_groups=mesh['row'=16,'col'=8] {'col'}, dimensions={0}, use_global_device_ids=true | all-gather | bytes 884736 | tf_op jit(solution)/shard_map/all_gather | solution.py:40
  23.3 0.8 fusion.19
  24.1 0.8 fusion.20
  25.0 2.2 bitcast_multiply_fusion.6
  27.2 3.8 %fusion.12 = f32[384,3328]{1,0:T(8,128)} fusion(bf16[512,3328]{1,0:T(8,128)(2,1)S(1)} %bitcast_multiply_fusion.6, bf16[384,1024]{1,0:T(8,128)(2,1)S(1)} %all_gather.3), kind=kOutput, calls=%fused_computation.24 | convolution fusion | flops 1308622848 | bytes 8912896 | tf_op jit(solution)/shard_map/dot_general | solution.py:66
  31.1 0.2 bitcast_multiply_fusion.7
  31.3 1.7 copy-done
  33.1 3.7 %fusion.14 = f32[384,3328]{1,0:T(8,128)} fusion(bf16[512,3328]{1,0:T(8,128)(2,1)S(1)} %bitcast_multiply_fusion.7, bf16[384,1024]{1,0:T(8,128)(2,1)S(1)} %all_gather.3), kind=kOutput, calls=%fused_computation.26 | convolution fusion | flops 1308622848 | bytes 8912896 | tf_op jit(solution)/shard_map/dot_general | solution.py:65
  36.8 0.7 copy-done.13
  37.7 2.3 bitcast_multiply_fusion.5
  40.0 1.5 fusion.8
  41.6 0.2 copy-done.2
  41.7 101.4 %all_to_all.24 = f32[16,24,3328]{2,1,0:T(8,128)} all-to-all(f32[16,24,3328]{2,1,0:T(8,128)S(1)} %fusion.8), channel_id=1, replica_groups=mesh['row'=16,'col'=8] {'row'}, dimensions={0} | all-to-all | bytes 10223616 | tf_op jit(solution)/shard_map/all_to_all | solution.py:73
  143.1 3.5 %reduce_sum.18 = f32[24,3328]{1,0:T(8,128)} reduce(f32[16,24,3328]{2,1,0:T(8,128)} %all_to_all.24, f32[]{:T(128)} %constant.1.clone.1), dimensions={0}, to_apply=%region_2.0 | reduce | flops 1198080 | bytes 5431300 | tf_op jit(solution)/shard_map/reduce_sum | solution.py:74
  146.7 1.3 broadcast_in_dim.27
  148.0 74.3 %all_to_all.25 = f32[16,24,3328]{2,1,0:T(8,128)} all-to-all(f32[16,24,3328]{2,1,0:T(8,128)S(1)} %broadcast_in_dim.27), channel_id=1, replica_groups=mesh['row'=16,'col'=8] {'row'}, dimensions={0} | all-to-all | bytes 10223616 | tf_op jit(solution)/shard_map/all_to_all | solution.py:76
  222.3 74.8 %all-reduce.3.cloned.1.call-done = (f32[384,3328]{1,0:T(8,128)}, f32[384,3328]{1,0:T(8,128)}) async-done(((f32[384,3328]{1,0:T(8,128)}, f32[384,3328]{1,0:T(8,128)}), (f32[384,3328]{1,0:T(8,128)}, f32[384,3328]{1,0:T(8,128)})) %all-reduce.3.cloned.1.call-update) | async-done | bytes 10223632 | tf_op jit(solution)/shard_map/psum | solution.py:63
  297.0 7.0 %multiply_convert_fusion = (bf16[384,3328]{1,0:T(8,128)(2,1)S(1)}, bf16[384,3328]{1,0:T(8,128)(2,1)S(1)}, bf16[384,3328]{1,0:T(8,128)(2,1)S(1)}) fusion(f32[384,3328]{1,0:T(8,128)} %get-tuple-element.5, f32[384,3328]{1,0:T(8,128)} %get-tuple-element.6, f32[16,24,3328]{2,1,0:T(8,128)} %all_to_all.25), kind=kLoop, calls=%fused_computation.12 | loop fusion | flops 19169280 | bytes 23003136 | tf_op jit(solution)/shard_map/convert_element_type | solution.py:79
  304.1 1.5 fusion.22
  305.7 1.0 copy-done.6
  306.7 1.9 copy-done.3
  308.6 1.5 fusion.21
  310.1 1.5 convolution_add_fusion
  311.6 1.3 pad_maximum_fusion
  312.9 5.9 %all-to-all-start.2 = ((f32[8,48,1024]{2,1,0:T(8,128)}), f32[8,48,1024]{2,1,0:T(8,128)}, u32[]{:S(2)}, u32[]{:S(2)}) async-start(f32[8,48,1024]{2,1,0:T(8,128)} %bitcast.73), calls=%async_computation.2 | async-start | bytes 3145728 | tf_op jit(solution)/shard_map/all_to_all | solution.py:94
  319.3 3.7 %fusion = bf16[3328,512]{1,0:T(8,128)(2,1)} fusion(bf16[384,3328]{1,0:T(8,128)(2,1)S(1)} %copy-done.7, f32[26,512]{1,0:T(8,128)S(1)} %bitcast.74, bf16[384,1024]{1,0:T(8,128)(2,1)S(1)} %copy-done.5), kind=kOutput, calls=%fused_computation.1 | convolution fusion | flops 1312030720 | bytes 6422528 | tf_op jit(solution)/shard_map/dot_general | solution.py:33
  323.1 3.7 %fusion.1 = bf16[512,3328]{1,0:T(8,128)(2,1)} fusion(bf16[384,3328]{1,0:T(8,128)(2,1)S(1)} %copy-done.11, f32[4,3328]{1,0:T(4,128)S(1)} %bitcast.76, bf16[384,1024]{1,0:T(8,128)(2,1)S(1)} %copy-done.5), kind=kOutput, calls=%fused_computation.3 | convolution fusion | flops 1312030720 | bytes 6410240 | tf_op jit(solution)/shard_map/dot_general | solution.py:33
  326.8 3.7 %fusion.2 = bf16[512,3328]{1,0:T(8,128)(2,1)} fusion(bf16[384,3328]{1,0:T(8,128)(2,1)S(1)} %copy-done.9, f32[4,3328]{1,0:T(4,128)S(1)} %bitcast.77, bf16[384,1024]{1,0:T(8,128)(2,1)S(1)} %copy-done.5), kind=kOutput, calls=%fused_computation.5 | convolution fusion | flops 1312030720 | bytes 6410240 | tf_op jit(solution)/shard_map/dot_general | solution.py:33
  330.5 9.0 %all-to-all-done.2 = f32[8,48,1024]{2,1,0:T(8,128)} async-done(((f32[8,48,1024]{2,1,0:T(8,128)}), f32[8,48,1024]{2,1,0:T(8,128)}, u32[]{:S(2)}, u32[]{:S(2)}) %all-to-all-start.2) | async-done | bytes 1572896 | tf_op jit(solution)/shard_map/all_to_all | solution.py:94
  339.5 1.5 reduce_sum.19
  341.1 0.6 fusion.17
  (44 shorter events, 1.0 us)
Async XLA Ops:
  7.2 289.9 %all-reduce.3.cloned.1.call-start = ((), (), s32[]{:S(2)}) async-start(), calls=%async_computation.3 | async-start | bytes 20447232 | tf_op jit(solution)/shard_map/psum | solution.py:63
  23.3 8.0 %copy-start.4 = (bf16[384,1024]{1,0:T(8,128)(2,1)}, bf16[384,1024]{1,0:T(8,128)(2,1)S(1)}, u32[]{:S(2)}) copy-start(bf16[384,1024]{1,0:T(8,128)(2,1)S(1)} %all_gather.3) | copy-start | bytes 2359300
  27.2 3.8 %copy-start.12 = (bf16[512,3328]{1,0:T(8,128)(2,1)S(1)}, bf16[512,3328]{1,0:T(8,128)(2,1)}, u32[]{:S(2)}) copy-start(bf16[512,3328]{1,0:T(8,128)(2,1)} %param.9) | copy-start | bytes 10223620
  31.3 1.8 copy-start
  36.8 0.7 copy-start.13
  37.7 2.3 slice-start
  40.0 1.8 copy-start.2
  297.0 7.1 %copy-start.1 = (bf16[512,3328]{1,0:T(8,128)(2,1)S(1)}, bf16[512,3328]{1,0:T(8,128)(2,1)}, u32[]{:S(2)}) copy-start(bf16[512,3328]{1,0:T(8,128)(2,1)} %copy-done) | copy-start | bytes 10223620
  304.1 1.6 copy-start.8
  304.1 2.6 copy-start.6
  304.1 6.0 %copy-start.10 = (bf16[384,3328]{1,0:T(8,128)(2,1)}, bf16[384,3328]{1,0:T(8,128)(2,1)S(1)}, u32[]{:S(2)}) copy-start(bf16[384,3328]{1,0:T(8,128)(2,1)S(1)} %get-tuple-element.9) | copy-start | bytes 7667716
  304.1 4.5 %copy-start.3 = (bf16[3328,512]{1,0:T(8,128)(2,1)S(1)}, bf16[3328,512]{1,0:T(8,128)(2,1)}, u32[]{:S(2)}) copy-start(bf16[3328,512]{1,0:T(8,128)(2,1)} %copy-done.2) | copy-start | bytes 10223620
  311.6 7.7 %copy-start.5 = (bf16[384,1024]{1,0:T(8,128)(2,1)S(1)}, bf16[384,1024]{1,0:T(8,128)(2,1)}, u32[]{:S(2)}) copy-start(bf16[384,1024]{1,0:T(8,128)(2,1)} %copy-done.4) | copy-start | bytes 2359300
  311.6 7.7 %copy-start.7 = (bf16[384,3328]{1,0:T(8,128)(2,1)S(1)}, bf16[384,3328]{1,0:T(8,128)(2,1)}, u32[]{:S(2)}) copy-start(bf16[384,3328]{1,0:T(8,128)(2,1)} %copy-done.6) | copy-start | bytes 7667716
  312.9 26.6 %all-to-all-start.2 = ((f32[8,48,1024]{2,1,0:T(8,128)}), f32[8,48,1024]{2,1,0:T(8,128)}, u32[]{:S(2)}, u32[]{:S(2)}) async-start(f32[8,48,1024]{2,1,0:T(8,128)} %bitcast.73), calls=%async_computation.2 | async-start | bytes 3145728 | tf_op jit(solution)/shard_map/all_to_all | solution.py:94
  319.1 4.0 %copy-start.11 = (bf16[384,3328]{1,0:T(8,128)(2,1)S(1)}, bf16[384,3328]{1,0:T(8,128)(2,1)}, u32[]{:S(2)}) copy-start(bf16[384,3328]{1,0:T(8,128)(2,1)} %copy-done.10) | copy-start | bytes 7667716
  323.1 3.7 %copy-start.9 = (bf16[384,3328]{1,0:T(8,128)(2,1)S(1)}, bf16[384,3328]{1,0:T(8,128)(2,1)}, u32[]{:S(2)}) copy-start(bf16[384,3328]{1,0:T(8,128)(2,1)} %copy-done.8) | copy-start | bytes 7667716
Sparse Core Ops, SparseCore 0:
  36.9 260.0 all-reduce.2

commit v9 on v7

--- a/solution.py
+++ b/solution.py
@@ -37,9 +37,12 @@
 
 def body(tokens, gate_weight, up_weight, down_weight, gate_mask, up_mask, down_mask, out_grad):
     feat = tokens.shape[1]
-    both_all = lax.all_gather(
-        jnp.concatenate([tokens, out_grad], axis=1), "col", axis=0, tiled=True
+    both = jnp.concatenate([tokens, out_grad], axis=1)
+    peers = lax.axis_size("col")
+    both_rep = jnp.broadcast_to(both[None], (peers,) + both.shape).reshape(
+        peers * both.shape[0], both.shape[1]
     )
+    both_all = lax.all_to_all(both_rep, "col", 0, 0, tiled=True)
     tok_all = both_all[:, :feat]
     grad_all = both_all[:, feat:]
     width = gate_weight.shape[1]

time: 302 us -> 301 us (level)
  blocking collectives: 15.2 us -> 0 us
  matrix products: 27.2 us -> 34.5 us
  starting transfers between devices: 5.29 us -> 11.2 us
  other arithmetic: 14.8 us -> 19.3 us
    all_gather x1 -> x0, blocking collectives: 15.2 us -> none  [body(): lax.all_gather(jnp.concatenate([tokens, out_grad], axis=1), 'col', axis=0...]
    all_to_all x0 -> x1, starting transfers between devices: none -> 5.96 us  [body(): both_all = lax.all_to_all(both_rep, 'col', 0, 0, tiled=True)]
    mul x3, other arithmetic: 2.68 us -> 6.33 us  [expand_flat(): return (blocks * kept[:, None, :]).reshape(rows_v, cols_v)]
    dot_general x3, matrix products: 11.2 us -> 14.4 us  [contract_first(): lax.dot_general(left, right, (((0,), (0,)), ((), ())), preferred_element_...]
    all_to_all x1, waiting for transfers between devices: 8.98 us -> 5.75 us  [body(): spread = lax.all_to_all(both_part, 'col', 0, 0, tiled=True)]
    unnamed x44 -> x34, local copies, waits for them, and re-layouts: 7.15 us -> 4.66 us
  transfers between devices with their start and end apart: 2 -> 3, of which waited for: 2 -> 3; matrix products, arithmetic and copies ran while one was open for 4% -> 8% of each run, Pallas kernels for 0% -> 0%
where the time goes in v9:
time: 301 us; the launch traced here: 300 us
  waiting for transfers between devices  214 us (71%)
  matrix products  34.5 us (11%)
  other arithmetic  19.3 us (6%)
  between operations  14.3 us (5%)
  starting transfers between devices  11.2 us (4%)
  local copies, waits for them, and re-layouts  6.65 us (2%)
    psum x1, waiting for transfers between devices, body(): gate_val, up_val, hidden_grad = lax.psum(partial, 'row')  207 us
    dot_general x3, matrix products, contract_first(): lax.dot_general(left, right, (((0,), (0,)), ((), ())), preferred_element_...  14.4 us
    dot_general x3, matrix products, contract_last(): lax.dot_general(left, right, (((1,), (1,)), ((), ())), preferred_element_...  9.07 us
    convert_element_type x1, other arithmetic, body(): hidden = (silu_gate * up_val).astype(jnp.bfloat16)  7.04 us
    mul x3, other arithmetic, expand_flat(): return (blocks * kept[:, None, :]).reshape(rows_v, cols_v)  6.33 us
  transfers between devices with their start and end apart: 3, of which 3 were waited for; matrix products, arithmetic and copies ran while one was open for 8% of the time, Pallas kernels for 0%

profile of v9, /device:TPU:1, one launch (start us, length us, event | category | flops | bytes accessed | tf_op | source)
XLA Modules:
  0.0 300.2 jit_solution(2769118390925551863)
XLA Ops:
  7.2 0.8 pad_maximum_fusion.1
  8.0 1.0 broadcast_in_dim.24
  9.0 6.0 %all-to-all-start = ((bf16[8,48,1024]{2,1,0:T(8,128)(2,1)}), bf16[8,48,1024]{2,1,0:T(8,128)(2,1)}, u32[]{:S(2)}, u32[]{:S(2)}) async-start(bf16[8,48,1024]{2,1,0:T(8,128)(2,1)} %broadcast_in_dim.24), calls=%async_computation | async-start | bytes 1572864 | tf_op jit(solution)/shard_map/all_to_all | solution.py:45
  14.9 0.8 fusion.14
  15.7 0.8 fusion.16
  16.5 0.1 copy.15
  16.6 0.1 broadcast_in_dim.27
  16.8 0.8 fusion.15
  17.7 4.1 %bitcast_multiply_fusion.3 = bf16[3328,512]{1,0:T(8,128)(2,1)} fusion(bf16[3328,512]{1,0:T(8,128)(2,1)} %param.11, bf16[26,512]{1,0:T(8,128)(2,1)S(1)} %bitcast.63), kind=kLoop, calls=%fused_computation.11 | loop fusion | flops 1703936 | bytes 6842368 | tf_op jit(solution)/shard_map/mul | solution.py:23
  21.8 2.0 bitcast_multiply_fusion.5
  23.8 1.2 copy-done.10
  25.0 0.2 bitcast_multiply_fusion.4
  25.2 1.9 all-to-all-done
  27.2 6.1 %fusion.5 = f32[384,3328]{1,0:T(8,128)} fusion(bf16[3328,512]{1,0:T(8,128)(2,1)} %bitcast_multiply_fusion.3, bf16[384,1024]{1,0:T(8,128)(2,1)} %bitcast), kind=kOutput, calls=%fused_computation.17 | convolution fusion | flops 1308622848 | bytes 8912896 | tf_op jit(solution)/shard_map/dot_general | solution.py:27
  33.3 4.7 %fusion.11 = f32[384,3328]{1,0:T(8,128)} fusion(bf16[512,3328]{1,0:T(8,128)(2,1)S(1)} %copy-done, bf16[384,1024]{1,0:T(8,128)(2,1)} %bitcast), kind=kOutput, calls=%fused_computation.23 | convolution fusion | flops 1308622848 | bytes 8912896 | tf_op jit(solution)/shard_map/dot_general | solution.py:68
  38.0 4.9 %fusion.9 = f32[384,3328]{1,0:T(8,128)} fusion(bf16[512,3328]{1,0:T(8,128)(2,1)S(1)} %bitcast_multiply_fusion.4, bf16[384,1024]{1,0:T(8,128)(2,1)} %bitcast), kind=kOutput, calls=%fused_computation.21 | convolution fusion | flops 1308622848 | bytes 8912896 | tf_op jit(solution)/shard_map/dot_general | solution.py:69
  42.8 206.5 %all-reduce.3.cloned.1.call-done = (f32[384,3328]{1,0:T(8,128)}, f32[384,3328]{1,0:T(8,128)}, f32[384,3328]{1,0:T(8,128)}) async-done(((f32[384,3328]{1,0:T(8,128)}, f32[384,3328]{1,0:T(8,128)}, f32[384,3328]{1,0:T(8,128)}), (f32[384,3328]{1,0:T(8,128)}, f32[384,3328]{1,0:T(8,128)}, f32[384,3328]{1,0:T(8,128)})) %all-reduce.3.cloned.1.call-update) | async-done | bytes 15335440 | tf_op jit(solution)/shard_map/psum | solution.py:74
  249.4 7.0 %multiply_convert_fusion.2 = (bf16[384,3328]{1,0:T(8,128)(2,1)S(1)}, bf16[384,3328]{1,0:T(8,128)(2,1)S(1)}, bf16[384,3328]{1,0:T(8,128)(2,1)S(1)}) fusion(f32[384,3328]{1,0:T(8,128)} %get-tuple-element.7, f32[384,3328]{1,0:T(8,128)} %get-tuple-element.5, f32[384,3328]{1,0:T(8,128)} %get-tuple-element.6), kind=kLoop, calls=%fused_computation.8 | loop fusion | flops 19169280 | bytes 23003136 | tf_op jit(solution)/shard_map/convert_element_type | solution.py:78
  256.5 1.5 fusion.18
  258.0 1.0 copy-done.3
  259.0 1.9 copy-done.2
  260.9 1.5 fusion.17
  262.4 1.5 convolution_add_fusion
  263.9 1.3 pad_maximum_fusion
  265.3 5.3 %all-to-all-start.1 = ((f32[8,48,1024]{2,1,0:T(8,128)}), f32[8,48,1024]{2,1,0:T(8,128)}, u32[]{:S(2)}, u32[]{:S(2)}) async-start(f32[8,48,1024]{2,1,0:T(8,128)} %bitcast.58), calls=%async_computation.1 | async-start | bytes 3145728 | tf_op jit(solution)/shard_map/all_to_all | solution.py:93
  270.5 0.1 copy.16
  271.0 4.9 %fusion = bf16[3328,512]{1,0:T(8,128)(2,1)} fusion(bf16[384,3328]{1,0:T(8,128)(2,1)S(1)} %copy-done.4, f32[26,512]{1,0:T(8,128)S(1)} %bitcast.59, bf16[384,1024]{1,0:T(8,128)(2,1)} %bitcast), kind=kOutput, calls=%fused_computation.1 | convolution fusion | flops 1312030720 | bytes 6410240 | tf_op jit(solution)/shard_map/dot_general | solution.py:33
  275.9 4.9 %fusion.1 = bf16[512,3328]{1,0:T(8,128)(2,1)} fusion(bf16[384,3328]{1,0:T(8,128)(2,1)S(1)} %copy-done.8, f32[4,3328]{1,0:T(4,128)S(1)} %bitcast.61, bf16[384,1024]{1,0:T(8,128)(2,1)} %bitcast), kind=kOutput, calls=%fused_computation.3 | convolution fusion | flops 1312030720 | bytes 6410240 | tf_op jit(solution)/shard_map/dot_general | solution.py:33
  280.7 4.7 %fusion.2 = bf16[512,3328]{1,0:T(8,128)(2,1)} fusion(bf16[384,3328]{1,0:T(8,128)(2,1)S(1)} %copy-done.6, f32[4,3328]{1,0:T(4,128)S(1)} %bitcast.62, bf16[384,1024]{1,0:T(8,128)(2,1)} %bitcast), kind=kOutput, calls=%fused_computation.5 | convolution fusion | flops 1312030720 | bytes 6410240 | tf_op jit(solution)/shard_map/dot_general | solution.py:33
  285.5 5.7 %all-to-all-done.1 = f32[8,48,1024]{2,1,0:T(8,128)} async-done(((f32[8,48,1024]{2,1,0:T(8,128)}), f32[8,48,1024]{2,1,0:T(8,128)}, u32[]{:S(2)}, u32[]{:S(2)}) %all-to-all-start.1) | async-done | bytes 1572896 | tf_op jit(solution)/shard_map/all_to_all | solution.py:93
  291.2 1.5 reduce_sum.9
  292.7 0.6 fusion.13
  (34 shorter events, 0.6 us)
Async XLA Ops:
  9.0 18.2 %all-to-all-start = ((bf16[8,48,1024]{2,1,0:T(8,128)(2,1)}), bf16[8,48,1024]{2,1,0:T(8,128)(2,1)}, u32[]{:S(2)}, u32[]{:S(2)}) async-start(bf16[8,48,1024]{2,1,0:T(8,128)(2,1)} %broadcast_in_dim.24), calls=%async_computation | async-start | bytes 1572864 | tf_op jit(solution)/shard_map/all_to_all | solution.py:45
  14.9 234.4 %all-reduce.3.cloned.1.call-start = ((), (), s32[]{:S(2)}) async-start(), calls=%async_computation.2 | async-start | bytes 30670848 | tf_op jit(solution)/shard_map/psum | solution.py:74
  17.7 4.1 %copy-start.9 = (bf16[512,3328]{1,0:T(8,128)(2,1)S(1)}, bf16[512,3328]{1,0:T(8,128)(2,1)}, u32[]{:S(2)}) copy-start(bf16[512,3328]{1,0:T(8,128)(2,1)} %param.9) | copy-start | bytes 10223620
  21.8 3.2 %copy-start.10 = (bf16[512,3328]{1,0:T(8,128)(2,1)S(1)}, bf16[512,3328]{1,0:T(8,128)(2,1)}, u32[]{:S(2)}) copy-start(bf16[512,3328]{1,0:T(8,128)(2,1)} %param.10) | copy-start | bytes 10223620
  27.2 6.1 %copy-start = (bf16[512,3328]{1,0:T(8,128)(2,1)S(1)}, bf16[512,3328]{1,0:T(8,128)(2,1)}, u32[]{:S(2)}) copy-start(bf16[512,3328]{1,0:T(8,128)(2,1)} %bitcast_multiply_fusion.5) | copy-start | bytes 10223620
  249.4 7.1 %copy-start.1 = (bf16[512,3328]{1,0:T(8,128)(2,1)S(1)}, bf16[512,3328]{1,0:T(8,128)(2,1)}, u32[]{:S(2)}) copy-start(bf16[512,3328]{1,0:T(8,128)(2,1)} %bitcast_multiply_fusion.5) | copy-start | bytes 10223620
  256.4 1.6 copy-start.5
  256.4 2.6 copy-start.3
  256.4 6.0 %copy-start.7 = (bf16[384,3328]{1,0:T(8,128)(2,1)}, bf16[384,3328]{1,0:T(8,128)(2,1)S(1)}, u32[]{:S(2)}) copy-start(bf16[384,3328]{1,0:T(8,128)(2,1)S(1)} %get-tuple-element.10) | copy-start | bytes 7667716
  256.5 4.5 %copy-start.2 = (bf16[3328,512]{1,0:T(8,128)(2,1)S(1)}, bf16[3328,512]{1,0:T(8,128)(2,1)}, u32[]{:S(2)}) copy-start(bf16[3328,512]{1,0:T(8,128)(2,1)} %bitcast_multiply_fusion.3) | copy-start | bytes 10223620
  263.9 7.1 %copy-start.4 = (bf16[384,3328]{1,0:T(8,128)(2,1)S(1)}, bf16[384,3328]{1,0:T(8,128)(2,1)}, u32[]{:S(2)}) copy-start(bf16[384,3328]{1,0:T(8,128)(2,1)} %copy-done.3) | copy-start | bytes 7667716
  265.3 25.9 %all-to-all-start.1 = ((f32[8,48,1024]{2,1,0:T(8,128)}), f32[8,48,1024]{2,1,0:T(8,128)}, u32[]{:S(2)}, u32[]{:S(2)}) async-start(f32[8,48,1024]{2,1,0:T(8,128)} %bitcast.58), calls=%async_computation.1 | async-start | bytes 3145728 | tf_op jit(solution)/shard_map/all_to_all | solution.py:93
  270.7 5.1 %copy-start.8 = (bf16[384,3328]{1,0:T(8,128)(2,1)S(1)}, bf16[384,3328]{1,0:T(8,128)(2,1)}, u32[]{:S(2)}) copy-start(bf16[384,3328]{1,0:T(8,128)(2,1)} %copy-done.7) | copy-start | bytes 7667716
  275.9 4.9 %copy-start.6 = (bf16[384,3328]{1,0:T(8,128)(2,1)S(1)}, bf16[384,3328]{1,0:T(8,128)(2,1)}, u32[]{:S(2)}) copy-start(bf16[384,3328]{1,0:T(8,128)(2,1)} %copy-done.5) | copy-start | bytes 7667716
Sparse Core Ops, SparseCore 0:
  43.0 206.3 all-reduce.2

commit v10 on v9

--- a/solution.py
+++ b/solution.py
@@ -91,9 +91,9 @@
     both_part = jnp.concatenate([mixed_part, input_part], axis=1)
     ways = lax.axis_size("col")
     spread = lax.all_to_all(both_part, "col", 0, 0, tiled=True)
-    out_sums = spread.reshape(ways, spread.shape[0] // ways, spread.shape[1]).sum(axis=0)
-    mixed_out = out_sums[:, :feat].astype(jnp.bfloat16)
-    input_grad = out_sums[:, feat:].astype(jnp.bfloat16)
+    blocks = spread.reshape(ways, spread.shape[0] // ways, spread.shape[1])
+    mixed_out = blocks[:, :, :feat].sum(axis=0).astype(jnp.bfloat16)
+    input_grad = blocks[:, :, feat:].sum(axis=0).astype(jnp.bfloat16)
     grad_gate = jnp.concatenate(gate_parts, axis=1)
     grad_up = jnp.concatenate(up_parts, axis=1)
     grad_down = jnp.concatenate(down_parts, axis=0)

time: 301 us -> 301 us (level)
  no operation moved by 1% of the time
where the time goes in v10:
time: 301 us; the launch traced here: 300 us
  waiting for transfers between devices  214 us (71%)
  matrix products  34.6 us (11%)
  other arithmetic  19.9 us (7%)
  between operations  14.3 us (5%)
  starting transfers between devices  11.2 us (4%)
  local copies, waits for them, and re-layouts  6.01 us (2%)
    psum x1, waiting for transfers between devices, body(): gate_val, up_val, hidden_grad = lax.psum(partial, 'row')  207 us
    dot_general x3, matrix products, contract_first(): lax.dot_general(left, right, (((0,), (0,)), ((), ())), preferred_element_...  14.4 us
    dot_general x3, matrix products, contract_last(): lax.dot_general(left, right, (((1,), (1,)), ((), ())), preferred_element_...  9.08 us
    convert_element_type x1, other arithmetic, body(): hidden = (silu_gate * up_val).astype(jnp.bfloat16)  7.04 us
    mul x3, other arithmetic, expand_flat(): return (blocks * kept[:, None, :]).reshape(rows_v, cols_v)  6.33 us
  transfers between devices with their start and end apart: 3, of which 3 were waited for; matrix products, arithmetic and copies ran while one was open for 8% of the time, Pallas kernels for 0%

profile of v10, /device:TPU:1, one launch (start us, length us, event | category | flops | bytes accessed | tf_op | source)
XLA Modules:
  0.0 300.2 jit_solution(4658716182089684838)
XLA Ops:
  7.2 0.8 pad_maximum_fusion.1
  8.0 1.0 broadcast_in_dim.24
  9.0 6.0 %all-to-all-start = ((bf16[8,48,1024]{2,1,0:T(8,128)(2,1)}), bf16[8,48,1024]{2,1,0:T(8,128)(2,1)}, u32[]{:S(2)}, u32[]{:S(2)}) async-start(bf16[8,48,1024]{2,1,0:T(8,128)(2,1)} %broadcast_in_dim.24), calls=%async_computation | async-start | bytes 1572864 | tf_op jit(solution)/shard_map/all_to_all | solution.py:45
  14.9 0.8 fusion.13
  15.7 0.8 fusion.15
  16.5 0.1 copy.15
  16.6 0.1 broadcast_in_dim.27
  16.8 0.8 fusion.14
  17.6 0.1 broadcast_bitcast_fusion.2
  17.7 4.1 %bitcast_multiply_fusion.3 = bf16[3328,512]{1,0:T(8,128)(2,1)} fusion(bf16[3328,512]{1,0:T(8,128)(2,1)} %param.11, bf16[26,512]{1,0:T(8,128)(2,1)S(1)} %bitcast.63), kind=kLoop, calls=%fused_computation.11 | loop fusion | flops 1703936 | bytes 6842368 | tf_op jit(solution)/shard_map/mul | solution.py:23
  21.8 2.0 bitcast_multiply_fusion.5
  23.8 1.2 copy-done.10
  25.0 0.2 bitcast_multiply_fusion.4
  25.2 1.9 all-to-all-done
  27.2 6.0 %fusion.5 = f32[384,3328]{1,0:T(8,128)} fusion(bf16[3328,512]{1,0:T(8,128)(2,1)} %bitcast_multiply_fusion.3, bf16[384,1024]{1,0:T(8,128)(2,1)} %bitcast), kind=kOutput, calls=%fused_computation.19 | convolution fusion | flops 1308622848 | bytes 8912896 | tf_op jit(solution)/shard_map/dot_general | solution.py:27
  33.2 4.7 %fusion.11 = f32[384,3328]{1,0:T(8,128)} fusion(bf16[512,3328]{1,0:T(8,128)(2,1)S(1)} %copy-done, bf16[384,1024]{1,0:T(8,128)(2,1)} %bitcast), kind=kOutput, calls=%fused_computation.25 | convolution fusion | flops 1308622848 | bytes 8912896 | tf_op jit(solution)/shard_map/dot_general | solution.py:68
  38.0 4.9 %fusion.9 = f32[384,3328]{1,0:T(8,128)} fusion(bf16[512,3328]{1,0:T(8,128)(2,1)S(1)} %bitcast_multiply_fusion.4, bf16[384,1024]{1,0:T(8,128)(2,1)} %bitcast), kind=kOutput, calls=%fused_computation.23 | convolution fusion | flops 1308622848 | bytes 8912896 | tf_op jit(solution)/shard_map/dot_general | solution.py:69
  42.8 206.5 %all-reduce.3.cloned.1.call-done = (f32[384,3328]{1,0:T(8,128)}, f32[384,3328]{1,0:T(8,128)}, f32[384,3328]{1,0:T(8,128)}) async-done(((f32[384,3328]{1,0:T(8,128)}, f32[384,3328]{1,0:T(8,128)}, f32[384,3328]{1,0:T(8,128)}), (f32[384,3328]{1,0:T(8,128)}, f32[384,3328]{1,0:T(8,128)}, f32[384,3328]{1,0:T(8,128)})) %all-reduce.3.cloned.1.call-update) | async-done | bytes 15335440 | tf_op jit(solution)/shard_map/psum | solution.py:74
  249.4 7.0 %multiply_convert_fusion.2 = (bf16[384,3328]{1,0:T(8,128)(2,1)S(1)}, bf16[384,3328]{1,0:T(8,128)(2,1)S(1)}, bf16[384,3328]{1,0:T(8,128)(2,1)S(1)}) fusion(f32[384,3328]{1,0:T(8,128)} %get-tuple-element.9, f32[384,3328]{1,0:T(8,128)} %get-tuple-element.7, f32[384,3328]{1,0:T(8,128)} %get-tuple-element.8), kind=kLoop, calls=%fused_computation.8 | loop fusion | flops 19169280 | bytes 23003136 | tf_op jit(solution)/shard_map/convert_element_type | solution.py:78
  256.5 1.5 fusion.17
  258.0 1.0 copy-done.3
  259.0 1.9 copy-done.2
  260.9 1.5 fusion.16
  262.4 1.5 convolution_add_fusion
  264.0 1.3 pad_maximum_fusion
  265.3 5.3 %all-to-all-start.1 = ((f32[8,48,1024]{2,1,0:T(8,128)}), f32[8,48,1024]{2,1,0:T(8,128)}, u32[]{:S(2)}, u32[]{:S(2)}) async-start(f32[8,48,1024]{2,1,0:T(8,128)} %bitcast.58), calls=%async_computation.1 | async-start | bytes 3145728 | tf_op jit(solution)/shard_map/all_to_all | solution.py:93
  270.5 0.1 copy.16
  271.0 4.9 %fusion = bf16[3328,512]{1,0:T(8,128)(2,1)} fusion(bf16[384,3328]{1,0:T(8,128)(2,1)S(1)} %copy-done.4, f32[26,512]{1,0:T(8,128)S(1)} %bitcast.59, bf16[384,1024]{1,0:T(8,128)(2,1)} %bitcast), kind=kOutput, calls=%fused_computation.1 | convolution fusion | flops 1312030720 | bytes 6410240 | tf_op jit(solution)/shard_map/dot_general | solution.py:33
  275.9 4.9 %fusion.1 = bf16[512,3328]{1,0:T(8,128)(2,1)} fusion(bf16[384,3328]{1,0:T(8,128)(2,1)S(1)} %copy-done.8, f32[4,3328]{1,0:T(4,128)S(1)} %bitcast.61, bf16[384,1024]{1,0:T(8,128)(2,1)} %bitcast), kind=kOutput, calls=%fused_computation.3 | convolution fusion | flops 1312030720 | bytes 6410240 | tf_op jit(solution)/shard_map/dot_general | solution.py:33
  280.7 4.7 %fusion.2 = bf16[512,3328]{1,0:T(8,128)(2,1)} fusion(bf16[384,3328]{1,0:T(8,128)(2,1)S(1)} %copy-done.6, f32[4,3328]{1,0:T(4,128)S(1)} %bitcast.62, bf16[384,1024]{1,0:T(8,128)(2,1)} %bitcast), kind=kOutput, calls=%fused_computation.5 | convolution fusion | flops 1312030720 | bytes 6410240 | tf_op jit(solution)/shard_map/dot_general | solution.py:33
  285.5 5.7 %all-to-all-done.1 = f32[8,48,1024]{2,1,0:T(8,128)} async-done(((f32[8,48,1024]{2,1,0:T(8,128)}), f32[8,48,1024]{2,1,0:T(8,128)}, u32[]{:S(2)}, u32[]{:S(2)}) %all-to-all-start.1) | async-done | bytes 1572896 | tf_op jit(solution)/shard_map/all_to_all | solution.py:93
  291.2 2.2 slice_reduce_fusion
  (33 shorter events, 0.5 us)
Async XLA Ops:
  9.0 18.2 %all-to-all-start = ((bf16[8,48,1024]{2,1,0:T(8,128)(2,1)}), bf16[8,48,1024]{2,1,0:T(8,128)(2,1)}, u32[]{:S(2)}, u32[]{:S(2)}) async-start(bf16[8,48,1024]{2,1,0:T(8,128)(2,1)} %broadcast_in_dim.24), calls=%async_computation | async-start | bytes 1572864 | tf_op jit(solution)/shard_map/all_to_all | solution.py:45
  14.9 234.4 %all-reduce.3.cloned.1.call-start = ((), (), s32[]{:S(2)}) async-start(), calls=%async_computation.2 | async-start | bytes 30670848 | tf_op jit(solution)/shard_map/psum | solution.py:74
  17.7 4.1 %copy-start.9 = (bf16[512,3328]{1,0:T(8,128)(2,1)S(1)}, bf16[512,3328]{1,0:T(8,128)(2,1)}, u32[]{:S(2)}) copy-start(bf16[512,3328]{1,0:T(8,128)(2,1)} %param.9) | copy-start | bytes 10223620
  21.8 3.2 %copy-start.10 = (bf16[512,3328]{1,0:T(8,128)(2,1)S(1)}, bf16[512,3328]{1,0:T(8,128)(2,1)}, u32[]{:S(2)}) copy-start(bf16[512,3328]{1,0:T(8,128)(2,1)} %param.10) | copy-start | bytes 10223620
  27.2 6.1 %copy-start = (bf16[512,3328]{1,0:T(8,128)(2,1)S(1)}, bf16[512,3328]{1,0:T(8,128)(2,1)}, u32[]{:S(2)}) copy-start(bf16[512,3328]{1,0:T(8,128)(2,1)} %bitcast_multiply_fusion.5) | copy-start | bytes 10223620
  249.4 7.1 %copy-start.1 = (bf16[512,3328]{1,0:T(8,128)(2,1)S(1)}, bf16[512,3328]{1,0:T(8,128)(2,1)}, u32[]{:S(2)}) copy-start(bf16[512,3328]{1,0:T(8,128)(2,1)} %bitcast_multiply_fusion.5) | copy-start | bytes 10223620
  256.4 1.6 copy-start.5
  256.4 2.6 copy-start.3
  256.4 6.0 %copy-start.7 = (bf16[384,3328]{1,0:T(8,128)(2,1)}, bf16[384,3328]{1,0:T(8,128)(2,1)S(1)}, u32[]{:S(2)}) copy-start(bf16[384,3328]{1,0:T(8,128)(2,1)S(1)} %get-tuple-element.12) | copy-start | bytes 7667716
  256.5 4.5 %copy-start.2 = (bf16[3328,512]{1,0:T(8,128)(2,1)S(1)}, bf16[3328,512]{1,0:T(8,128)(2,1)}, u32[]{:S(2)}) copy-start(bf16[3328,512]{1,0:T(8,128)(2,1)} %bitcast_multiply_fusion.3) | copy-start | bytes 10223620
  264.0 7.1 %copy-start.4 = (bf16[384,3328]{1,0:T(8,128)(2,1)S(1)}, bf16[384,3328]{1,0:T(8,128)(2,1)}, u32[]{:S(2)}) copy-start(bf16[384,3328]{1,0:T(8,128)(2,1)} %copy-done.3) | copy-start | bytes 7667716
  265.3 25.9 %all-to-all-start.1 = ((f32[8,48,1024]{2,1,0:T(8,128)}), f32[8,48,1024]{2,1,0:T(8,128)}, u32[]{:S(2)}, u32[]{:S(2)}) async-start(f32[8,48,1024]{2,1,0:T(8,128)} %bitcast.58), calls=%async_computation.1 | async-start | bytes 3145728 | tf_op jit(solution)/shard_map/all_to_all | solution.py:93
  270.7 5.1 %copy-start.8 = (bf16[384,3328]{1,0:T(8,128)(2,1)S(1)}, bf16[384,3328]{1,0:T(8,128)(2,1)}, u32[]{:S(2)}) copy-start(bf16[384,3328]{1,0:T(8,128)(2,1)} %copy-done.7) | copy-start | bytes 7667716
  275.9 4.9 %copy-start.6 = (bf16[384,3328]{1,0:T(8,128)(2,1)S(1)}, bf16[384,3328]{1,0:T(8,128)(2,1)}, u32[]{:S(2)}) copy-start(bf16[384,3328]{1,0:T(8,128)(2,1)} %copy-done.5) | copy-start | bytes 7667716
Sparse Core Ops, SparseCore 0:
  43.0 206.3 all-reduce.2

commit v11 on v9

--- a/solution.py
+++ b/solution.py
@@ -53,7 +53,6 @@
     gate_parts, up_parts, down_parts = [], [], []
     mixed_part = None
     input_part = None
-    prev_sums = None
     for k in range(CHUNKS):
         t0, t1 = bounds[k], bounds[k + 1]
         h0, h1 = t0 * tile, t1 * tile
@@ -64,15 +63,16 @@
         w_up = expand_flat(up_weight[:, h0:h1], u_mask)
         w_down = expand_flat(down_weight[h0:h1, :], d_mask)
         n = h1 - h0
-        partial = (
-            jnp.dot(tok_all, w_gate, preferred_element_type=jnp.float32),
-            jnp.dot(tok_all, w_up, preferred_element_type=jnp.float32),
-            contract_last(grad_all, w_down),
+        w_pair = jnp.concatenate([w_gate, w_up], axis=1)
+        pair_val, hidden_grad = lax.psum(
+            (
+                jnp.dot(tok_all, w_pair, preferred_element_type=jnp.float32),
+                contract_last(grad_all, w_down),
+            ),
+            "row",
         )
-        if prev_sums is not None:
-            partial, _ = lax.optimization_barrier((partial, prev_sums))
-        gate_val, up_val, hidden_grad = lax.psum(partial, "row")
-        prev_sums = gate_val
+        gate_val = pair_val[:, :n]
+        up_val = pair_val[:, n:]
         sigmoid_gate = jax.nn.sigmoid(gate_val)
         silu_gate = gate_val * sigmoid_gate
         hidden = (silu_gate * up_val).astype(jnp.bfloat16)

time: 301 us -> 295 us (0.980)
  matrix products: 34.5 us -> 30.5 us
    dot_general x2 -> x1, matrix products: 9.56 us -> 6.59 us  [body(): jnp.dot(tok_all, w_pair, preferred_element_type=jnp.float32)]
    mul x3 -> x2, other arithmetic: 6.33 us -> 5.71 us  [expand_flat(): return (blocks * kept[:, None, :]).reshape(rows_v, cols_v)]
where the time goes in v11:
time: 295 us
  waiting for transfers between devices  214 us (73%)
  matrix products  30.5 us (10%)
  other arithmetic  18.7 us (6%)
  between operations  14.3 us (5%)
  starting transfers between devices  11.2 us (4%)
  local copies, waits for them, and re-layouts  5.56 us (2%)
    psum x1, waiting for transfers between devices, body(): lax.psum((jnp.dot(tok_all, w_pair, preferred_element_type=jnp.float32), c...  206 us
    dot_general x3, matrix products, contract_first(): lax.dot_general(left, right, (((0,), (0,)), ((), ())), preferred_element_...  14.4 us
    dot_general x3, matrix products, contract_last(): lax.dot_general(left, right, (((1,), (1,)), ((), ())), preferred_element_...  8.04 us
    convert_element_type x1, other arithmetic, body(): up_grad = (hidden_grad * silu_gate).astype(jnp.bfloat16)  7.04 us
    dot_general x1, matrix products, body(): jnp.dot(tok_all, w_pair, preferred_element_type=jnp.float32)  6.59 us
    all_to_all x1, starting transfers between devices, body(): both_all = lax.all_to_all(both_rep, 'col', 0, 0, tiled=True)  5.96 us
  transfers between devices with their start and end apart: 3, of which 3 were waited for; matrix products, arithmetic and copies ran while one was open for 8% of the time, Pallas kernels for 0%

profile of v11, /device:TPU:1, one launch (start us, length us, event | category | flops | bytes accessed | tf_op | source)
XLA Modules:
  0.0 294.6 jit_solution(11016286749695407911)
XLA Ops:
  7.2 0.8 pad_maximum_fusion.1
  8.0 1.0 broadcast_in_dim.24
  9.0 6.0 %all-to-all-start = ((bf16[8,48,1024]{2,1,0:T(8,128)(2,1)}), bf16[8,48,1024]{2,1,0:T(8,128)(2,1)}, u32[]{:S(2)}, u32[]{:S(2)}) async-start(bf16[8,48,1024]{2,1,0:T(8,128)(2,1)} %broadcast_in_dim.24), calls=%async_computation | async-start | bytes 1572864 | tf_op jit(solution)/shard_map/all_to_all | solution.py:45
  14.9 0.8 fusion.17
  15.7 0.1 broadcast_bitcast_fusion.2
  15.8 0.8 fusion.18
  16.7 0.8 fusion.16
  17.4 0.1 copy.15
  17.6 0.1 broadcast_in_dim.27
  17.7 2.4 bitcast_multiply_fusion.3
  20.1 0.6 copy-done.6
  20.7 1.0 copy-done.7
  21.7 3.4 %bitcast_multiply_fusion.4 = (bf16[512,3328]{1,0:T(8,128)(2,1)}, bf16[512,3328]{1,0:T(8,128)(2,1)}) fusion(bf16[512,3328]{1,0:T(8,128)(2,1)S(1)} %copy-done.6, bf16[4,3328]{1,0:T(4,128)(2,1)S(1)} %bitcast.63, bf16[512,3328]{1,0:T(8,128)(2,1)S(1)} %copy-done.7, bf16[4,3328]{1,0:T(4,128)(2,1)S(1)} %bitcast.64), kind=kLoop, calls=%fused_computation.16 | loop fusion | flops 3407872 | bytes 13684736 | tf_op jit(solution)/shard_map/mul | solution.py:23
  25.1 2.1 all-to-all-done
  27.2 5.0 %fusion.9 = f32[384,3328]{1,0:T(8,128)} fusion(bf16[3328,512]{1,0:T(8,128)(2,1)S(1)} %bitcast_multiply_fusion.3, bf16[384,1024]{1,0:T(8,128)(2,1)} %bitcast), kind=kOutput, calls=%fused_computation.21 | convolution fusion | flops 1308622848 | bytes 8912896 | tf_op jit(solution)/shard_map/dot_general | solution.py:27
  32.2 6.6 %fusion = f32[384,6656]{1,0:T(8,128)} fusion(bf16[512,3328]{1,0:T(8,128)(2,1)S(1)} %copy-done.8, bf16[512,3328]{1,0:T(8,128)(2,1)S(1)} %copy-done.10, bf16[384,1024]{1,0:T(8,128)(2,1)} %bitcast), kind=kOutput, calls=%fused_computation | convolution fusion | flops 2630877184 | bytes 17432576 | tf_op jit(solution)/shard_map/dot_general | solution.py:69
  38.8 206.5 %all-reduce.3.cloned.1.call-done = (f32[384,3328]{1,0:T(8,128)}, f32[384,6656]{1,0:T(8,128)}) async-done(((f32[384,3328]{1,0:T(8,128)}, f32[384,6656]{1,0:T(8,128)}), (f32[384,3328]{1,0:T(8,128)}, f32[384,6656]{1,0:T(8,128)})) %all-reduce.3.cloned.1.call-update) | async-done | bytes 15335440 | tf_op jit(solution)/shard_map/psum | solution.py:67
  245.3 7.0 %multiply_convert_fusion = (bf16[384,3328]{1,0:T(8,128)(2,1)S(1)}, bf16[384,3328]{1,0:T(8,128)(2,1)S(1)}, bf16[384,3328]{1,0:T(8,128)(2,1)S(1)}) fusion(f32[384,3328]{1,0:T(8,128)} %get-tuple-element.5, f32[384,6656]{1,0:T(8,128)} %get-tuple-element.6), kind=kLoop, calls=%fused_computation.10 | loop fusion | flops 19169280 | bytes 23003136 | tf_op jit(solution)/shard_map/convert_element_type | solution.py:82
  252.4 1.5 fusion.20
  253.9 0.8 copy-done
  254.7 1.5 fusion.19
  256.2 0.6 copy-done.9
  256.8 1.5 convolution_add_fusion
  258.3 1.3 pad_maximum_fusion
  259.6 5.3 %all-to-all-start.1 = ((f32[8,48,1024]{2,1,0:T(8,128)}), f32[8,48,1024]{2,1,0:T(8,128)}, u32[]{:S(2)}, u32[]{:S(2)}) async-start(f32[8,48,1024]{2,1,0:T(8,128)} %bitcast.56), calls=%async_computation.1 | async-start | bytes 3145728 | tf_op jit(solution)/shard_map/all_to_all | solution.py:93
  264.9 0.1 copy.16
  265.4 4.9 %fusion.4 = bf16[3328,512]{1,0:T(8,128)(2,1)} fusion(bf16[384,3328]{1,0:T(8,128)(2,1)S(1)} %copy-done.1, f32[26,512]{1,0:T(8,128)S(1)} %bitcast.57, bf16[384,1024]{1,0:T(8,128)(2,1)} %bitcast), kind=kOutput, calls=%fused_computation.5 | convolution fusion | flops 1312030720 | bytes 6410240 | tf_op jit(solution)/shard_map/dot_general | solution.py:33
  270.2 4.9 %fusion.5 = bf16[512,3328]{1,0:T(8,128)(2,1)} fusion(bf16[384,3328]{1,0:T(8,128)(2,1)S(1)} %copy-done.5, f32[4,3328]{1,0:T(4,128)S(1)} %bitcast.59, bf16[384,1024]{1,0:T(8,128)(2,1)} %bitcast), kind=kOutput, calls=%fused_computation.7 | convolution fusion | flops 1312030720 | bytes 6410240 | tf_op jit(solution)/shard_map/dot_general | solution.py:33
  275.1 4.7 %fusion.6 = bf16[512,3328]{1,0:T(8,128)(2,1)} fusion(bf16[384,3328]{1,0:T(8,128)(2,1)S(1)} %copy-done.3, f32[4,3328]{1,0:T(4,128)S(1)} %bitcast.60, bf16[384,1024]{1,0:T(8,128)(2,1)} %bitcast), kind=kOutput, calls=%fused_computation.9 | convolution fusion | flops 1312030720 | bytes 6410240 | tf_op jit(solution)/shard_map/dot_general | solution.py:33
  279.8 5.7 %all-to-all-done.1 = f32[8,48,1024]{2,1,0:T(8,128)} async-done(((f32[8,48,1024]{2,1,0:T(8,128)}), f32[8,48,1024]{2,1,0:T(8,128)}, u32[]{:S(2)}, u32[]{:S(2)}) %all-to-all-start.1) | async-done | bytes 1572896 | tf_op jit(solution)/shard_map/all_to_all | solution.py:93
  285.6 1.5 reduce_sum.9
  287.1 0.6 fusion.15
  (34 shorter events, 0.5 us)
Async XLA Ops:
  9.0 18.2 %all-to-all-start = ((bf16[8,48,1024]{2,1,0:T(8,128)(2,1)}), bf16[8,48,1024]{2,1,0:T(8,128)(2,1)}, u32[]{:S(2)}, u32[]{:S(2)}) async-start(bf16[8,48,1024]{2,1,0:T(8,128)(2,1)} %broadcast_in_dim.24), calls=%async_computation | async-start | bytes 1572864 | tf_op jit(solution)/shard_map/all_to_all | solution.py:45
  14.9 230.4 %all-reduce.3.cloned.1.call-start = ((), (), s32[]{:S(2)}) async-start(), calls=%async_computation.2 | async-start | bytes 30670848 | tf_op jit(solution)/shard_map/psum | solution.py:67
  17.7 3.0 %copy-start.6 = (bf16[512,3328]{1,0:T(8,128)(2,1)S(1)}, bf16[512,3328]{1,0:T(8,128)(2,1)}, u32[]{:S(2)}) copy-start(bf16[512,3328]{1,0:T(8,128)(2,1)} %param.10) | copy-start | bytes 10223620
  17.7 4.0 %copy-start.7 = (bf16[512,3328]{1,0:T(8,128)(2,1)S(1)}, bf16[512,3328]{1,0:T(8,128)(2,1)}, u32[]{:S(2)}) copy-start(bf16[512,3328]{1,0:T(8,128)(2,1)} %param.9) | copy-start | bytes 10223620
  27.2 5.0 %copy-start.8 = (bf16[512,3328]{1,0:T(8,128)(2,1)S(1)}, bf16[512,3328]{1,0:T(8,128)(2,1)}, u32[]{:S(2)}) copy-start(bf16[512,3328]{1,0:T(8,128)(2,1)} %get-tuple-element.18) | copy-start | bytes 10223620
  27.2 5.0 %copy-start.10 = (bf16[512,3328]{1,0:T(8,128)(2,1)S(1)}, bf16[512,3328]{1,0:T(8,128)(2,1)}, u32[]{:S(2)}) copy-start(bf16[512,3328]{1,0:T(8,128)(2,1)} %get-tuple-element.19) | copy-start | bytes 10223620
  245.3 7.1 %copy-start.11 = (bf16[512,3328]{1,0:T(8,128)(2,1)S(1)}, bf16[512,3328]{1,0:T(8,128)(2,1)}, u32[]{:S(2)}) copy-start(bf16[512,3328]{1,0:T(8,128)(2,1)} %get-tuple-element.19) | copy-start | bytes 10223620
  252.3 1.6 copy-start.2
  252.4 2.3 copy-start
  252.4 3.8 %copy-start.4 = (bf16[384,3328]{1,0:T(8,128)(2,1)}, bf16[384,3328]{1,0:T(8,128)(2,1)S(1)}, u32[]{:S(2)}) copy-start(bf16[384,3328]{1,0:T(8,128)(2,1)S(1)} %get-tuple-element.7) | copy-start | bytes 7667716
  254.7 2.1 copy-start.9
  258.3 7.1 %copy-start.1 = (bf16[384,3328]{1,0:T(8,128)(2,1)S(1)}, bf16[384,3328]{1,0:T(8,128)(2,1)}, u32[]{:S(2)}) copy-start(bf16[384,3328]{1,0:T(8,128)(2,1)} %copy-done) | copy-start | bytes 7667716
  259.6 25.9 %all-to-all-start.1 = ((f32[8,48,1024]{2,1,0:T(8,128)}), f32[8,48,1024]{2,1,0:T(8,128)}, u32[]{:S(2)}, u32[]{:S(2)}) async-start(f32[8,48,1024]{2,1,0:T(8,128)} %bitcast.56), calls=%async_computation.1 | async-start | bytes 3145728 | tf_op jit(solution)/shard_map/all_to_all | solution.py:93
  265.1 5.1 %copy-start.5 = (bf16[384,3328]{1,0:T(8,128)(2,1)S(1)}, bf16[384,3328]{1,0:T(8,128)(2,1)}, u32[]{:S(2)}) copy-start(bf16[384,3328]{1,0:T(8,128)(2,1)} %copy-done.4) | copy-start | bytes 7667716
  270.2 4.9 %copy-start.3 = (bf16[384,3328]{1,0:T(8,128)(2,1)S(1)}, bf16[384,3328]{1,0:T(8,128)(2,1)}, u32[]{:S(2)}) copy-start(bf16[384,3328]{1,0:T(8,128)(2,1)} %copy-done.2) | copy-start | bytes 7667716
Sparse Core Ops, SparseCore 0:
  39.0 206.2 all-reduce.2

commit v12 on v11

--- a/solution.py
+++ b/solution.py
@@ -84,7 +84,7 @@
         up_parts.append(expand_flat(contract_first(tok_all, up_grad), u_mask).astype(jnp.bfloat16))
         down_parts.append(expand_flat(contract_first(hidden, grad_all), d_mask).astype(jnp.bfloat16))
         m = jnp.dot(hidden, w_down, preferred_element_type=jnp.float32)
-        i = contract_last(gate_grad, w_gate) + contract_last(up_grad, w_up)
+        i = contract_last(jnp.concatenate([gate_grad, up_grad], axis=1), w_pair)
         mixed_part = m if mixed_part is None else mixed_part + m
         input_part = i if input_part is None else input_part + i
 

time: 295 us -> 298 us (1.010)
    dot_general x3 -> x2, matrix products: 8.04 us -> 7.84 us  [contract_last(): lax.dot_general(left, right, (((1,), (1,)), ((), ())), preferred_element_...]
where the time goes in v12:
time: 298 us; the launch traced here: 297 us
  waiting for transfers between devices  214 us (72%)
  matrix products  30.3 us (10%)
  other arithmetic  18.5 us (6%)
  between operations  14.2 us (5%)
  starting transfers between devices  11.2 us (4%)
  local copies, waits for them, and re-layouts  8.33 us (3%)
    psum x1, waiting for transfers between devices, body(): lax.psum((jnp.dot(tok_all, w_pair, preferred_element_type=jnp.float32), c...  206 us
    dot_general x3, matrix products, contract_first(): lax.dot_general(left, right, (((0,), (0,)), ((), ())), preferred_element_...  14.4 us
    dot_general x2, matrix products, contract_last(): lax.dot_general(left, right, (((1,), (1,)), ((), ())), preferred_element_...  7.84 us
    convert_element_type x1, other arithmetic, body(): gate_grad = (hidden_grad * up_val * sigmoid_gate * (1.0 + gate_val * (1.0...  6.9 us
    dot_general x1, matrix products, body(): jnp.dot(tok_all, w_pair, preferred_element_type=jnp.float32)  6.59 us
    unnamed x36, local copies, waits for them, and re-layouts  6.33 us
  transfers between devices with their start and end apart: 3, of which 3 were waited for; matrix products, arithmetic and copies ran while one was open for 8% of the time, Pallas kernels for 0%

profile of v12, /device:TPU:1, one launch (start us, length us, event | category | flops | bytes accessed | tf_op | source)
XLA Modules:
  0.0 297.0 jit_solution(618047937860927063)
XLA Ops:
  7.2 0.8 pad_maximum_fusion.4
  8.0 1.0 broadcast_in_dim.24
  9.0 6.0 %all-to-all-start = ((bf16[8,48,1024]{2,1,0:T(8,128)(2,1)}), bf16[8,48,1024]{2,1,0:T(8,128)(2,1)}, u32[]{:S(2)}, u32[]{:S(2)}) async-start(bf16[8,48,1024]{2,1,0:T(8,128)(2,1)} %broadcast_in_dim.24), calls=%async_computation | async-start | bytes 1572864 | tf_op jit(solution)/shard_map/all_to_all | solution.py:45
  14.9 0.8 fusion.19
  15.8 0.8 fusion.20
  16.7 0.8 fusion.18
  17.4 0.1 copy.15
  17.6 0.1 broadcast_in_dim.27
  17.7 2.4 bitcast_multiply_fusion.3
  20.1 0.6 copy-done.6
  20.7 1.0 copy-done.7
  21.7 3.4 %bitcast_multiply_fusion.4 = (bf16[512,3328]{1,0:T(8,128)(2,1)}, bf16[512,3328]{1,0:T(8,128)(2,1)}) fusion(bf16[512,3328]{1,0:T(8,128)(2,1)S(1)} %copy-done.6, bf16[4,3328]{1,0:T(4,128)(2,1)S(1)} %bitcast.59, bf16[512,3328]{1,0:T(8,128)(2,1)S(1)} %copy-done.7, bf16[4,3328]{1,0:T(4,128)(2,1)S(1)} %bitcast.60), kind=kLoop, calls=%fused_computation.18 | loop fusion | flops 3407872 | bytes 13684736 | tf_op jit(solution)/shard_map/mul | solution.py:23
  25.1 2.1 all-to-all-done
  27.2 5.0 %fusion.10 = f32[384,3328]{1,0:T(8,128)} fusion(bf16[3328,512]{1,0:T(8,128)(2,1)S(1)} %bitcast_multiply_fusion.3, bf16[384,1024]{1,0:T(8,128)(2,1)} %bitcast), kind=kOutput, calls=%fused_computation.22 | convolution fusion | flops 1308622848 | bytes 8912896 | tf_op jit(solution)/shard_map/dot_general | solution.py:27
  32.2 6.6 %fusion.8 = f32[384,6656]{1,0:T(8,128)} fusion(bf16[512,3328]{1,0:T(8,128)(2,1)S(1)} %copy-done.8, bf16[512,3328]{1,0:T(8,128)(2,1)S(1)} %copy-done.10, bf16[384,1024]{1,0:T(8,128)(2,1)} %bitcast), kind=kOutput, calls=%fused_computation.16 | convolution fusion | flops 2630877184 | bytes 17432576 | tf_op jit(solution)/shard_map/dot_general | solution.py:69
  38.8 206.5 %all-reduce.3.cloned.1.call-done = (f32[384,3328]{1,0:T(8,128)}, f32[384,6656]{1,0:T(8,128)}) async-done(((f32[384,3328]{1,0:T(8,128)}, f32[384,6656]{1,0:T(8,128)}), (f32[384,3328]{1,0:T(8,128)}, f32[384,6656]{1,0:T(8,128)})) %all-reduce.3.cloned.1.call-update) | async-done | bytes 15335440 | tf_op jit(solution)/shard_map/psum | solution.py:67
  245.3 6.9 %multiply_convert_fusion.1 = (bf16[384,3328]{1,0:T(8,128)(2,1)S(1)}, bf16[384,3328]{1,0:T(8,128)(2,1)S(1)}, bf16[384,3328]{1,0:T(8,128)(2,1)S(1)}) fusion(f32[384,3328]{1,0:T(8,128)} %get-tuple-element.5, f32[384,6656]{1,0:T(8,128)} %get-tuple-element.6), kind=kLoop, calls=%fused_computation.12 | loop fusion | flops 19169280 | bytes 23003136 | tf_op jit(solution)/shard_map/convert_element_type | solution.py:81
  252.3 1.5 fusion.21
  253.7 1.1 copy-done.2
  254.8 1.2 copy-done.4
  256.0 0.7 copy-done.9
  256.7 1.2 copy-done.11
  257.9 2.8 fusion.3
  260.7 1.3 pad_maximum_fusion.3
  262.0 5.3 %all-to-all-start.1 = ((f32[8,48,1024]{2,1,0:T(8,128)}), f32[8,48,1024]{2,1,0:T(8,128)}, u32[]{:S(2)}, u32[]{:S(2)}) async-start(f32[8,48,1024]{2,1,0:T(8,128)} %bitcast.52), calls=%async_computation.1 | async-start | bytes 3145728 | tf_op jit(solution)/shard_map/all_to_all | solution.py:93
  267.3 0.1 copy.16
  267.8 4.9 %fusion = bf16[3328,512]{1,0:T(8,128)(2,1)} fusion(bf16[384,3328]{1,0:T(8,128)(2,1)S(1)} %copy-done.1, f32[26,512]{1,0:T(8,128)S(1)} %bitcast.53, bf16[384,1024]{1,0:T(8,128)(2,1)} %bitcast), kind=kOutput, calls=%fused_computation.2 | convolution fusion | flops 1312030720 | bytes 6410240 | tf_op jit(solution)/shard_map/dot_general | solution.py:33
  272.6 4.9 %fusion.1 = bf16[512,3328]{1,0:T(8,128)(2,1)} fusion(bf16[384,3328]{1,0:T(8,128)(2,1)S(1)} %copy-done.5, f32[4,3328]{1,0:T(4,128)S(1)} %bitcast.55, bf16[384,1024]{1,0:T(8,128)(2,1)} %bitcast), kind=kOutput, calls=%fused_computation.4 | convolution fusion | flops 1312030720 | bytes 6410240 | tf_op jit(solution)/shard_map/dot_general | solution.py:33
  277.5 4.7 %fusion.2 = bf16[512,3328]{1,0:T(8,128)(2,1)} fusion(bf16[384,3328]{1,0:T(8,128)(2,1)S(1)} %copy-done.3, f32[4,3328]{1,0:T(4,128)S(1)} %bitcast.56, bf16[384,1024]{1,0:T(8,128)(2,1)} %bitcast), kind=kOutput, calls=%fused_computation.6 | convolution fusion | flops 1312030720 | bytes 6410240 | tf_op jit(solution)/shard_map/dot_general | solution.py:33
  282.2 5.7 %all-to-all-done.1 = f32[8,48,1024]{2,1,0:T(8,128)} async-done(((f32[8,48,1024]{2,1,0:T(8,128)}), f32[8,48,1024]{2,1,0:T(8,128)}, u32[]{:S(2)}, u32[]{:S(2)}) %all-to-all-start.1) | async-done | bytes 1572896 | tf_op jit(solution)/shard_map/all_to_all | solution.py:93
  288.0 1.5 reduce_sum.9
  289.5 0.6 fusion.17
  (33 shorter events, 0.6 us)
Async XLA Ops:
  9.0 18.2 %all-to-all-start = ((bf16[8,48,1024]{2,1,0:T(8,128)(2,1)}), bf16[8,48,1024]{2,1,0:T(8,128)(2,1)}, u32[]{:S(2)}, u32[]{:S(2)}) async-start(bf16[8,48,1024]{2,1,0:T(8,128)(2,1)} %broadcast_in_dim.24), calls=%async_computation | async-start | bytes 1572864 | tf_op jit(solution)/shard_map/all_to_all | solution.py:45
  14.9 230.4 %all-reduce.3.cloned.1.call-start = ((), (), s32[]{:S(2)}) async-start(), calls=%async_computation.2 | async-start | bytes 30670848 | tf_op jit(solution)/shard_map/psum | solution.py:67
  17.7 3.0 %copy-start.6 = (bf16[512,3328]{1,0:T(8,128)(2,1)S(1)}, bf16[512,3328]{1,0:T(8,128)(2,1)}, u32[]{:S(2)}) copy-start(bf16[512,3328]{1,0:T(8,128)(2,1)} %param.10) | copy-start | bytes 10223620
  17.7 4.0 %copy-start.7 = (bf16[512,3328]{1,0:T(8,128)(2,1)S(1)}, bf16[512,3328]{1,0:T(8,128)(2,1)}, u32[]{:S(2)}) copy-start(bf16[512,3328]{1,0:T(8,128)(2,1)} %param.9) | copy-start | bytes 10223620
  27.2 5.0 %copy-start.8 = (bf16[512,3328]{1,0:T(8,128)(2,1)S(1)}, bf16[512,3328]{1,0:T(8,128)(2,1)}, u32[]{:S(2)}) copy-start(bf16[512,3328]{1,0:T(8,128)(2,1)} %get-tuple-element.18) | copy-start | bytes 10223620
  27.2 5.0 %copy-start.10 = (bf16[512,3328]{1,0:T(8,128)(2,1)S(1)}, bf16[512,3328]{1,0:T(8,128)(2,1)}, u32[]{:S(2)}) copy-start(bf16[512,3328]{1,0:T(8,128)(2,1)} %get-tuple-element.19) | copy-start | bytes 10223620
  252.2 1.5 copy-start
  252.2 2.6 copy-start.2
  252.2 3.8 %copy-start.4 = (bf16[384,3328]{1,0:T(8,128)(2,1)}, bf16[384,3328]{1,0:T(8,128)(2,1)S(1)}, u32[]{:S(2)}) copy-start(bf16[384,3328]{1,0:T(8,128)(2,1)S(1)} %get-tuple-element.8) | copy-start | bytes 7667716
  252.2 4.5 %copy-start.9 = (bf16[512,3328]{1,0:T(8,128)(2,1)S(1)}, bf16[512,3328]{1,0:T(8,128)(2,1)}, u32[]{:S(2)}) copy-start(bf16[512,3328]{1,0:T(8,128)(2,1)} %get-tuple-element.18) | copy-start | bytes 10223620
  252.2 5.7 %copy-start.11 = (bf16[512,3328]{1,0:T(8,128)(2,1)S(1)}, bf16[512,3328]{1,0:T(8,128)(2,1)}, u32[]{:S(2)}) copy-start(bf16[512,3328]{1,0:T(8,128)(2,1)} %get-tuple-element.19) | copy-start | bytes 10223620
  260.7 7.0 %copy-start.1 = (bf16[384,3328]{1,0:T(8,128)(2,1)S(1)}, bf16[384,3328]{1,0:T(8,128)(2,1)}, u32[]{:S(2)}) copy-start(bf16[384,3328]{1,0:T(8,128)(2,1)} %copy-done) | copy-start | bytes 7667716
  262.0 25.9 %all-to-all-start.1 = ((f32[8,48,1024]{2,1,0:T(8,128)}), f32[8,48,1024]{2,1,0:T(8,128)}, u32[]{:S(2)}, u32[]{:S(2)}) async-start(f32[8,48,1024]{2,1,0:T(8,128)} %bitcast.52), calls=%async_computation.1 | async-start | bytes 3145728 | tf_op jit(solution)/shard_map/all_to_all | solution.py:93
  267.5 5.1 %copy-start.5 = (bf16[384,3328]{1,0:T(8,128)(2,1)S(1)}, bf16[384,3328]{1,0:T(8,128)(2,1)}, u32[]{:S(2)}) copy-start(bf16[384,3328]{1,0:T(8,128)(2,1)} %copy-done.4) | copy-start | bytes 7667716
  272.6 4.9 %copy-start.3 = (bf16[384,3328]{1,0:T(8,128)(2,1)S(1)}, bf16[384,3328]{1,0:T(8,128)(2,1)}, u32[]{:S(2)}) copy-start(bf16[384,3328]{1,0:T(8,128)(2,1)} %copy-done.2) | copy-start | bytes 7667716
Sparse Core Ops, SparseCore 0:
  39.0 206.2 all-reduce.2
